TPU v7x, 512 devices: a whole 4x4x16 slice. The times are simulated.
512 devices in a mesh: gy: 16 (over x_hi, y, core), gx: 32 (over z, x_lo).
Axes of the slice: x: 4 (x_hi: 2, x_lo: 2; x = x_hi * 2 + x_lo), y: 4, z: 16, core: 2. Of those that a mesh axis runs over, the one named last changes fastest.
Arguments:
- embeddings: bfloat16 [128, 4096, 128], P('gy', 'gx'), may hold values from -180 to 180
- affinity: float32 [4, 128, 4096], P(None, 'gy', 'gx'), may hold values from 0 to 1, as said below
- assignment: int32 [128, 4096], P('gy', 'gx'), may hold values from 0 to 1023
Outputs:
- min_distance: float32 [128, 4096], P('gy', 'gx')
- new_centroids: float32 [1024, 128], replicated
Inputs may be any that keep to these rules, and one draw needn't show every extreme that they name: `affinity`: weight 0 exactly for edges that leave the slab; every other edge weighs 0.05 or more.
All inputs are finite; a program needn't handle non-finite values.
Results may differ from a plain program's by a relative error of at most 0.00045.
Values may be sent and summed in bfloat16 or wider, within the bound.
No kernel may reach another device: no remote copies, remote signals or barrier semaphores. Data moves between devices by JAX's collectives and lax.ppermute only.
A program may use at most 64 MiB of HBM per device.

v0:
```python
import math

import jax
import jax.numpy as jnp
from jax import lax
from jax.sharding import PartitionSpec as P

K = 1024
DEGREE = 4


COEFFS = (0.5, 0.45, 0.35, 0.25, 0.15)


def extended(block, sides, width):
    for axis, dim in sides:
        count = lax.axis_size(axis)
        forward = [(i, i + 1) for i in range(count - 1)]
        backward = [(target, source) for source, target in forward]
        low = lax.ppermute(
            lax.slice_in_dim(block, block.shape[dim] - width, None, axis=dim), axis, forward
        )
        high = lax.ppermute(lax.slice_in_dim(block, 0, width, axis=dim), axis, backward)
        block = jnp.concatenate([low, block, high], axis=dim)
    return block


def degree_of(w_ext):
    w_east, w_south, w_diag, w_anti = (w_ext[0], w_ext[1], w_ext[2], w_ext[3])
    result = w_east[1:-1, 1:-1] + w_east[1:-1, :-2]
    result = result + w_south[1:-1, 1:-1] + w_south[:-2, 1:-1]
    result = result + w_diag[1:-1, 1:-1] + w_diag[:-2, :-2]
    return result + w_anti[1:-1, 1:-1] + w_anti[:-2, 2:]


def edge_sum(w_ext, field):
    w_east, w_south, w_diag, w_anti = (w_ext[0], w_ext[1], w_ext[2], w_ext[3])
    result = w_east[1:-1, 1:-1, None] * field[1:-1, 2:]
    result = result + w_east[1:-1, :-2, None] * field[1:-1, :-2]
    result = result + w_south[1:-1, 1:-1, None] * field[2:, 1:-1]
    result = result + w_south[:-2, 1:-1, None] * field[:-2, 1:-1]
    result = result + w_diag[1:-1, 1:-1, None] * field[2:, 2:]
    result = result + w_diag[:-2, :-2, None] * field[:-2, :-2]
    result = result + w_anti[1:-1, 1:-1, None] * field[2:, :-2]
    return result + w_anti[:-2, 2:, None] * field[:-2, 2:]


def whitening(gram, count):
    lower = jnp.linalg.cholesky(gram)
    identity = jnp.eye(gram.shape[0], dtype=gram.dtype)
    inverse = jax.scipy.linalg.solve_triangular(lower, identity, lower=True)
    return math.sqrt(count) * inverse.T


def on_device(embeddings, affinity, assignment):
    rows, cols, chans = embeddings.shape
    reach_all = DEGREE
    w_width = 1
    w_ext = extended(affinity, (("gy", 1), ("gx", 2)), w_width)
    scale = lax.rsqrt(degree_of(w_ext))[..., None]

    def apply_each(field):
        padded = extended(scale * field, (("gy", 0), ("gx", 1)), 1)
        return scale * edge_sum(w_ext, padded)

    previous = embeddings.astype(jnp.float32)
    current = apply_each(previous)
    filtered = COEFFS[0] * previous + COEFFS[1] * current
    for order in range(2, reach_all + 1):
        following = 2.0 * apply_each(current) - previous
        previous, current = (current, following)
        filtered = filtered + COEFFS[order] * following
    pixels = rows * cols
    flat = filtered.reshape(pixels, chans)
    labels = assignment.reshape(pixels)
    total_pixels = pixels * lax.axis_size("gy") * lax.axis_size("gx")
    clusters = K
    block = 128
    highest = lax.Precision.HIGHEST
    gram_local = lax.dot_general(
        flat, flat, (((0,), (0,)), ((), ())), precision=highest, preferred_element_type=jnp.float32
    )
    gram = lax.psum(gram_local, ("gy", "gx"))
    transform = whitening(gram, total_pixels)
    whitened = jnp.dot(flat, transform, precision=highest, preferred_element_type=jnp.float32)

    def one_block(index):
        first = index * block
        onehot = (labels[:, None] == first + jnp.arange(block, dtype=jnp.int32)[None, :]).astype(
            jnp.float32
        )
        partial_sums = lax.dot_general(
            onehot,
            whitened,
            (((0,), (0,)), ((), ())),
            precision=highest,
            preferred_element_type=jnp.float32,
        )
        return (partial_sums, jnp.sum(onehot, axis=0))

    block_sums, block_counts = lax.map(one_block, jnp.arange(clusters // block, dtype=jnp.int32))
    local_sums = block_sums.reshape(clusters, chans)
    local_counts = block_counts.reshape(clusters)
    sums, counts = lax.psum((local_sums, local_counts), ("gy", "gx"))
    centroids = sums / (counts + 1.0)[:, None]
    norms = jnp.sum(whitened * whitened, axis=1)

    def nearest(index, best):
        centre_part = lax.dynamic_slice_in_dim(centroids, index * block, block, 0)
        cross = lax.dot_general(
            whitened,
            centre_part,
            (((1,), (1,)), ((), ())),
            precision=highest,
            preferred_element_type=jnp.float32,
        )
        part_norms = jnp.sum(centre_part * centre_part, axis=1)
        distance = (norms[:, None] - 2.0 * cross + part_norms[None, :]) / chans
        return jnp.minimum(best, jnp.min(distance, axis=1))

    best = lax.fori_loop(0, clusters // block, nearest, jnp.full((pixels,), jnp.inf, jnp.float32))
    return (best.reshape(rows, cols), centroids)


def solution(mesh):
    return jax.shard_map(
        on_device,
        mesh=mesh,
        in_specs=(P("gy", "gx", None), P(None, "gy", "gx"), P("gy", "gx")),
        out_specs=(P("gy", "gx"), P()),
        check_vma=False,
    )
```

profile of v0, /device:TPU:1, one launch (start us, length us, event | category | flops | bytes accessed | tf_op | source)
XLA Modules:
  0.0 1083.6 jit_solution(14910961055857017236)
XLA Ops:
  8.0 4.7 collective-permute-start
  12.7 5.6 collective-permute-start.1
  23.0 4.0 collective-permute-done.3
  27.4 2.8 collective-permute-start.4
  30.2 1.9 collective-permute-start.5
  32.1 3.6 collective-permute-done.5
  37.1 5.0 collective-permute-start.7
  44.7 2.7 collective-permute-start.8
  49.4 3.6 collective-permute-done.9
  54.4 5.2 collective-permute-start.11
  62.1 2.7 collective-permute-start.12
  66.7 4.6 collective-permute-done.13
  72.6 5.1 collective-permute-start.15
  80.4 2.7 collective-permute-start.16
  83.1 1.9 collective-permute-start.17
  85.0 7.7 collective-permute-done.17
  94.0 5.2 collective-permute-start.19
  103.6 466.6 %all-reduce.3.cloned.1.call-done = f32[128,128]{0,1:T(8,128)} async-done(((f32[128,128]{0,1:T(8,128)}), f32[128,128]{0,1:T(8,128)}) %all-reduce.3.cloned.1.call-update) | async-done | bytes 65552 | tf_op jit(solution)/shard_map/psum | solution.py:83
  571.3 11.7 %cholesky.14 = f32[128,128]{1,0:T(8,128)S(1)} custom-call(f32[128,128]{1,0:T(8,128)S(1)} %fusion.63), custom_call_target="Cholesky" | custom-call | tf_op jit(solution)/shard_map/jit(cholesky)/cholesky | solution.py:49
  584.3 9.8 custom-call.7
  595.7 23.2 %while.26 = (s32[]{:T(128)}, f32[8,128,128]{2,1,0:T(8,128)}, f32[8,128]{1,0:T(8,128)S(1)}, s32[8,128]{1,0:T(8,128)S(1)}, s32[8]{0:T(128)S(1)}, /*index=5*/f32[10...) while((s32[]{:T(128)}, f32[8,128,128]{2,1,0:T(8,128)}, f32[8,128]{1,0:T(8,128)S(1)}, ...), condition=%wide.region_5.6_spmd, body=%wide.region_3.5_spmd.sunk | while | flops 201850880 | bytes 601725 | solution.py:101
  618.9 101.7 %psum.23 = f32[1024]{0:T(1024)S(1)} all-reduce(f32[1024]{0:T(1024)S(1)} %bitcast.54), channel_id=1, replica_groups=mesh['gy'=16,'gx'=32] {'gy','gx'}, use_global_device_ids=true, to_apply=%region_7.8 | all-reduce | flops 1024 | bytes 8192 | tf_op jit(solution)/shard_map/psum | solution.py:104
  720.7 347.7 %all-reduce.5.cloned.1.call-done = f32[1024,128]{1,0:T(8,128)} async-done(((f32[1024,128]{1,0:T(8,128)}), f32[1024,128]{1,0:T(8,128)}) %all-reduce.5.cloned.1.call-update) | async-done | bytes 524304 | tf_op jit(solution)/shard_map/psum | solution.py:104
  1069.6 6.3 while.27
  (141 shorter events, 56.7 us)
Async XLA Ops:
  7.2 563.1 %all-reduce.3.cloned.1.call-start = ((), (), s32[]{:S(2)}) async-start(), calls=%async_computation | async-start | bytes 131072 | tf_op jit(solution)/shard_map/psum | solution.py:83
  8.0 19.0 %copy-start.5 = (f32[4,8,128]{2,1,0:T(8,128)S(1)}, f32[4,8,128]{2,1,0:T(8,128)}, u32[]{:S(2)}) copy-start(f32[4,8,128]{2,1,0:T(8,128)} %param.8) | copy-start | bytes 49156
  8.0 10.4 collective-permute-start
  12.7 14.5 %copy-start = (bf16[8,128,128]{2,1,0:T(8,128)(2,1)S(1)}, bf16[8,128,128]{2,1,0:T(8,128)(2,1)}, u32[]{:S(2)}) copy-start(bf16[8,128,128]{2,1,0:T(8,128)(2,1)} %param.7) | copy-start | bytes 786436
  12.7 6.4 collective-permute-start.1
  20.0 3.0 collective-permute-start.2
  21.7 5.3 collective-permute-start.3
  27.4 4.7 collective-permute-start.4
  30.2 5.6 collective-permute-start.5
  35.8 6.4 collective-permute-start.6
  37.1 5.8 collective-permute-start.7
  44.7 4.7 collective-permute-start.8
  47.5 5.6 collective-permute-start.9
  53.1 6.5 collective-permute-start.10
  54.4 5.9 collective-permute-start.11
  62.1 4.7 collective-permute-start.12
  64.8 6.5 collective-permute-start.13
  71.3 6.4 collective-permute-start.14
  72.6 5.9 collective-permute-start.15
  80.4 4.7 collective-permute-start.16
  83.1 9.6 collective-permute-start.17
  92.7 6.5 collective-permute-start.18
  94.0 5.9 collective-permute-start.19
  103.4 965.0 %all-reduce.5.cloned.1.call-start = ((), (), s32[]{:S(2)}) async-start(), calls=%async_computation.1 | async-start | bytes 1048576 | tf_op jit(solution)/shard_map/psum | solution.py:104
  (4 other events, 3.3 us)
Sparse Core Ops, SparseCore 0:
  103.5 466.6 all-reduce.2
  619.1 449.2 all-reduce.4
where the time goes:
time: 1090 us; the launch traced here: 1080 us
  waiting for transfers between devices  842 us (77%)
  blocking collectives  102 us (9%)
  starting transfers between devices  57.9 us (5%)
  other arithmetic  35.1 us (3%)
  matrix products  18.7 us (2%)
  between operations  14.5 us (1%)
    psum x1, waiting for transfers between devices, on_device(): gram = lax.psum(gram_local, ('gy', 'gx'))  467 us
    psum x1, waiting for transfers between devices, on_device(): sums, counts = lax.psum((local_sums, local_counts), ('gy', 'gx'))  348 us
    psum x1, blocking collectives, on_device(): sums, counts = lax.psum((local_sums, local_counts), ('gy', 'gx'))  102 us
    ppermute x10, starting transfers between devices, extended(): lax.ppermute(lax.slice_in_dim(block, block.shape[dim] - width, None, axis...  37.9 us
    ppermute x10, waiting for transfers between devices, extended(): lax.ppermute(lax.slice_in_dim(block, 0, width, axis=dim), axis, backward)  24.3 us
  transfers between devices with their start and end apart: 22, of which 12 were waited for; matrix products, arithmetic and copies ran while one was open for 0% of the time, Pallas kernels for 0%

commit v1 on v0

v1 whole, which is shorter than its diff:
```python
import functools
import math

import jax
import jax.numpy as jnp
from jax import lax
from jax.experimental import pallas as pl
from jax.experimental.pallas import tpu as pltpu
from jax.sharding import Mesh
from jax.sharding import PartitionSpec as P

K = 1024
C = 128
TH = 8
TW = 128
HALO = 4
COEFFS = (0.5, 0.45, 0.35, 0.25, 0.15)
PARTS = 32
BLOCK = 40
ROWS_OF = K // PARTS
F32 = jnp.float32
BF16 = jnp.bfloat16


def split3(x):
    high = x.astype(BF16)
    rest = x - high.astype(F32)
    mid = rest.astype(BF16)
    low = (rest - mid.astype(F32)).astype(BF16)
    return high, mid, low


def dot(a, b, dims):
    return lax.dot_general(a, b, (dims, ((), ())), preferred_element_type=F32)


def filter_kernel(
    xc_ref, xn_ref, xs_ref, xw_ref, xe_ref, wc_ref, ww_ref, we_ref, lab_ref,
    filt_ref, msg_ref, a_ref, b_ref, wb_ref, t_ref,
):
    zeros8 = jnp.zeros((16, 8, C), F32)
    for buf in (a_ref, b_ref):
        buf[:, 0:8, :] = zeros8
        buf[:, 152:160, :] = zeros8
    a_ref[:, 8:16, :] = xw_ref[...].astype(F32)
    a_ref[:, 144:152, :] = xe_ref[...].astype(F32)
    a_ref[0:4, 16:144, :] = xn_ref[...].astype(F32)
    a_ref[4:12, 16:144, :] = xc_ref[...].astype(F32)
    a_ref[12:16, 16:144, :] = xs_ref[...].astype(F32)

    lane = lax.broadcasted_iota(jnp.int32, (24, 128), 1)

    def weights(d):
        side = jnp.where(lane < 64, we_ref[d], ww_ref[d])
        return jnp.concatenate([wc_ref[d], side], axis=1)

    def right(x):
        return pltpu.roll(x, 255, 1)

    def left(x):
        return pltpu.roll(x, 1, 1)

    def down(x):
        return pltpu.roll(x, 23, 0)

    def up(x):
        return pltpu.roll(x, 1, 0)

    east, south, diag, anti = weights(0), weights(1), weights(2), weights(3)
    degree = east + left(east)
    degree = degree + south + up(south)
    degree = degree + diag + up(left(diag))
    degree = degree + anti + up(right(anti))
    scale = jnp.where(degree > 0.0, lax.rsqrt(jnp.where(degree > 0.0, degree, 1.0)), 0.0)
    below = down(scale)
    normed = (
        scale * east * right(scale),
        scale * south * below,
        scale * diag * right(below),
        scale * anti * left(below),
    )
    stack = jnp.concatenate(normed + (jnp.zeros((32, 256), F32),), axis=0)
    centre = stack[:, 0:128].T
    sides = stack[:, 128:256].T
    t_ref[0:8, :] = sides[120:128]
    t_ref[8:136, :] = centre
    t_ref[136:144, :] = sides[0:8]
    for d in range(4):
        for r in range(16):
            k = d * 24 + r + 4
            wb_ref[d, r, 0:8, :] = jnp.zeros((8, C), F32)
            wb_ref[d, r, 152:160, :] = jnp.zeros((8, C), F32)
            wb_ref[d, r, 8:152, :] = jnp.broadcast_to(t_ref[:, k:k + 1], (144, C))

    def apply_at(src, r, s, n):
        here, before, after = pl.ds(s, n), pl.ds(s - 1, n), pl.ds(s + 1, n)
        out = wb_ref[0, r, here, :] * src[r, after, :]
        out = out + wb_ref[0, r, before, :] * src[r, before, :]
        out = out + wb_ref[1, r, here, :] * src[r + 1, here, :]
        out = out + wb_ref[1, r - 1, here, :] * src[r - 1, here, :]
        out = out + wb_ref[2, r, here, :] * src[r + 1, after, :]
        out = out + wb_ref[2, r - 1, before, :] * src[r - 1, before, :]
        out = out + wb_ref[3, r, here, :] * src[r + 1, before, :]
        return out + wb_ref[3, r - 1, after, :] * src[r - 1, after, :]

    step = 24

    def first(r, carry):
        for s in range(8, 152, step):
            b_ref[r, s:s + step, :] = apply_at(a_ref, r, s, step)
        return carry

    def later(cur, prev):
        def body(r, carry):
            for s in range(8, 152, step):
                new = 2.0 * apply_at(cur, r, s, step) - prev[r, s:s + step, :]
                prev[r, s:s + step, :] = new
            return carry
        return body

    def accumulate(r, carry):
        for s in range(0, TW, 32):
            total = COEFFS[0] * a_ref[r + 4, 16 + s:48 + s, :] + COEFFS[1] * b_ref[r + 4, 16 + s:48 + s, :]
            filt_ref[pl.ds(r * TW + s, 32), :] = total
        return carry

    def add(src, coeff):
        def body(r, carry):
            for s in range(0, TW, 32):
                rows = pl.ds(r * TW + s, 32)
                filt_ref[rows, :] = filt_ref[rows, :] + coeff * src[r + 4, 16 + s:48 + s, :]
            return carry
        return body

    def last(r, carry):
        for s in range(0, TW, 16):
            here = pl.ds(s + 16, 16)
            new = 2.0 * apply_at(b_ref, r + 4, s + 16, 16) - a_ref[r + 4, here, :]
            rows = pl.ds(r * TW + s, 16)
            filt_ref[rows, :] = filt_ref[rows, :] + COEFFS[4] * new
        return carry

    lax.fori_loop(1, 15, first, 0)
    lax.fori_loop(0, TH, accumulate, 0)
    lax.fori_loop(2, 14, later(b_ref, a_ref), 0)
    lax.fori_loop(0, TH, add(a_ref, COEFFS[2]), 0)
    lax.fori_loop(3, 13, later(a_ref, b_ref), 0)
    lax.fori_loop(0, TH, add(b_ref, COEFFS[3]), 0)
    lax.fori_loop(0, TH, last, 0)

    high, mid, low = split3(filt_ref[...])
    tall = ((0,), (0,))
    by_high = dot(high, jnp.concatenate([high, mid, low], axis=1), tall)
    by_mid = dot(mid, jnp.concatenate([high, mid], axis=1), tall)
    by_low = dot(low, high, tall)
    gram = by_high[:, 2 * C:] + by_low + by_mid[:, C:]
    gram = gram + (by_high[:, C:2 * C] + by_mid[:, :C])
    gram = gram + by_high[:, :C]

    pieces = jnp.concatenate([high, mid, low], axis=1)
    ones = jnp.ones((8, TH * TW), BF16)
    chunk = 256
    for k0 in range(0, K, chunk):
        cluster = lax.broadcasted_iota(jnp.int32, (chunk, TW), 0) + k0
        onehot = jnp.concatenate(
            [(cluster == lab_ref[r:r + 1, :]).astype(F32).astype(BF16) for r in range(TH)], axis=1
        )
        part = dot(onehot, pieces, ((1,), (0,)))
        part = (part[:, 2 * C:] + part[:, C:2 * C]) + part[:, :C]
        counts = dot(ones, onehot, ((1,), (1,)))
        for q in range(chunk // ROWS_OF):
            p = k0 // ROWS_OF + q
            msg_ref[p, 0:ROWS_OF, :] = part[q * ROWS_OF:(q + 1) * ROWS_OF]
            msg_ref[p, ROWS_OF:ROWS_OF + 4, :] = gram[4 * p:4 * p + 4]
            lanes = (p * ROWS_OF - k0) // TW * TW
            msg_ref[p, ROWS_OF + 4:BLOCK, :] = counts[0:4, lanes:lanes + TW]


def run_filter(xc, xn, xs, xw, xe, wc, ww, we, labels):
    return pl.pallas_call(
        filter_kernel,
        out_shape=(
            jax.ShapeDtypeStruct((TH * TW, C), F32),
            jax.ShapeDtypeStruct((PARTS, BLOCK, C), F32),
        ),
        scratch_shapes=[
            pltpu.VMEM((16, 160, C), F32),
            pltpu.VMEM((16, 160, C), F32),
            pltpu.VMEM((4, 16, 160, C), F32),
            pltpu.VMEM((144, 128), F32),
        ],
        compiler_params=pltpu.CompilerParams(vmem_limit_bytes=40 * 2**20),
    )(xc, xn, xs, xw, xe, wc, ww, we, labels)


def finish_kernel(msg_ref, filt_ref, best_ref, cent_ref, g_ref, *, total):
    for p in range(PARTS):
        g_ref[4 * p:4 * p + 4, 0:C] = msg_ref[p, ROWS_OF:ROWS_OF + 4, :]
    row = lax.broadcasted_iota(jnp.int32, (C, C), 0)
    col = lax.broadcasted_iota(jnp.int32, (C, C), 1)
    g_ref[:, C:2 * C] = jnp.where(row == col, 1.0, 0.0).astype(F32)

    panel = 32
    sub = lax.broadcasted_iota(jnp.int32, (panel, 1), 0)
    for p0 in range(0, C, panel):
        left = g_ref[p0:p0 + panel, 0:C]
        right = g_ref[p0:p0 + panel, C:2 * C]
        for i in range(panel):
            j = p0 + i
            column = left[:, j:j + 1]
            pivot = left[i:i + 1, j:j + 1]
            root = lax.rsqrt(pivot)
            urow = left[i:i + 1, :] * root
            irow = right[i:i + 1, :] * root
            factor = jnp.where(sub > i, column * root, 0.0)
            keep = sub == i
            left = jnp.where(keep, urow, left - factor * urow)
            right = jnp.where(keep, irow, right - factor * irow)
        g_ref[p0:p0 + panel, 0:C] = left
        g_ref[p0:p0 + panel, C:2 * C] = right
        if p0 + panel < C:
            uh, um, ul = split3(left)
            full = jnp.concatenate([left, right], axis=1)
            fh, fm, fl = split3(full)
            lhs = jnp.concatenate([uh, um, ul, um, uh, uh], axis=0)
            rhs = jnp.concatenate([fl, fm, fh, fh, fm, fh], axis=0)
            update = dot(lhs, rhs, ((0,), (0,)))
            rest = slice(p0 + panel, C)
            g_ref[rest, :] = g_ref[rest, :] - update[p0 + panel:C, :]

    inverse = g_ref[:, C:2 * C] * math.sqrt(total)
    ih, im, il = split3(inverse)
    lhs = jnp.concatenate([il, im, ih, im, ih, ih], axis=1)

    def times_inverse(x, transposed):
        xh, xm, xl = split3(x)
        rhs = jnp.concatenate([xh, xm, xl, xh, xm, xh], axis=1)
        if transposed:
            return dot(lhs, rhs, ((1,), (1,)))
        return dot(rhs, lhs, ((1,), (1,)))

    whitened_t = times_inverse(filt_ref[...], True)
    norms = jnp.sum(whitened_t * whitened_t, axis=0, keepdims=True)
    wh, wm, wl = split3(whitened_t)
    w_all = jnp.concatenate([wl, wm, wh, wm, wh, wh], axis=0)
    best = None
    for b in range(K // C):
        sums = jnp.concatenate([msg_ref[4 * b + q, 0:ROWS_OF, :] for q in range(4)], axis=0)
        counts = jnp.broadcast_to(msg_ref[4 * b, ROWS_OF + 4:ROWS_OF + 5, :], (C, C)).T
        cent = times_inverse(sums, False) / (counts + 1.0)
        cent_ref[b * C:(b + 1) * C, :] = cent
        cent_norm = jnp.sum(cent * cent, axis=1, keepdims=True)
        ch, cm, cl = split3(-2.0 * cent)
        c_all = jnp.concatenate([ch, cm, cl, ch, cm, ch], axis=1)
        value = dot(c_all, w_all, ((1,), (0,))) + cent_norm
        low = jnp.min(value, axis=0, keepdims=True)
        best = low if best is None else jnp.minimum(best, low)
    result = (norms + best) / C
    for r in range(TH):
        best_ref[r:r + 1, :] = result[:, r * TW:(r + 1) * TW]


def run_finish(msg, filt, total):

    return pl.pallas_call(
        functools.partial(finish_kernel, total=total),
        out_shape=(
            jax.ShapeDtypeStruct((TH, TW), F32),
            jax.ShapeDtypeStruct((K, C), F32),
        ),
        scratch_shapes=[pltpu.VMEM((C, 2 * C), F32)],
        compiler_params=pltpu.CompilerParams(vmem_limit_bytes=40 * 2**20),
    )(msg, filt)


GY = ("xh", "y", "c")
GX = ("zh", "zl", "xl")


def shift(block, axes, size, forward):
    pairs = [(i, i + 1) for i in range(size - 1)]
    if not forward:
        pairs = [(b, a) for a, b in pairs]
    return lax.ppermute(block, axes, pairs)


def exchange(x, axes):
    return lax.all_to_all(x, axes, 0, 0)


def spread(x, axes, count):
    return exchange(jnp.broadcast_to(x[None], (count,) + x.shape), axes)


def reduce_all(msg):
    msg = jnp.sum(exchange(msg.reshape(2, PARTS // 2, BLOCK, C), "c"), axis=0)
    piece = jnp.sum(exchange(msg, ("xh", "y", "xl")), axis=0)
    piece = jnp.sum(spread(piece, "zl", 4), axis=0)
    piece = jnp.sum(spread(piece, "zh", 4), axis=0)
    half = spread(piece, ("xh", "y", "xl"), PARTS // 2)
    return lax.all_gather(half, "c", axis=0, tiled=True)


def on_device(embeddings, affinity, assignment):
    n_gy, n_gx = 16, 32
    xn = shift(embeddings[TH - HALO:], GY, n_gy, True)
    xs = shift(embeddings[:HALO], GY, n_gy, False)
    wn = shift(affinity, GY, n_gy, True)
    ws = shift(affinity, GY, n_gy, False)
    edge = jnp.concatenate([xn[:, TW - 8:], embeddings[:, TW - 8:], xs[:, TW - 8:]], axis=0)
    xw = shift(edge, GX, n_gx, True)
    edge = jnp.concatenate([xn[:, :8], embeddings[:, :8], xs[:, :8]], axis=0)
    xe = shift(edge, GX, n_gx, False)
    wc = jnp.concatenate([wn, affinity, ws], axis=1)
    ww = shift(wc, GX, n_gx, True)
    we = shift(wc, GX, n_gx, False)
    filt, msg = run_filter(embeddings, xn, xs, xw, xe, wc, ww, we, assignment)
    msg = reduce_all(msg)
    return run_finish(msg, filt, TH * TW * n_gy * n_gx)


def solution(mesh):
    inner = Mesh(mesh.devices.reshape(2, 4, 2, 4, 4, 2), GY + GX)
    return jax.shard_map(
        on_device,
        mesh=inner,
        in_specs=(P(GY, GX, None), P(None, GY, GX), P(GY, GX)),
        out_specs=(P(GY, GX), P()),
        check_vma=False,
    )
```

time: 1090 us -> 127 us (0.12)
  waiting for transfers between devices: 842 us -> 3.59 us
  other arithmetic: 35.1 us -> 0.09 us
  starting transfers between devices: 57.9 us -> 24.3 us
  blocking collectives: 102 us -> 73.7 us
  Pallas kernels: 0 us -> 22.4 us
  matrix products: 18.7 us -> 0 us
  between operations: 14.5 us -> 0.86 us
    psum x2 -> x0, waiting for transfers between devices: 814 us -> none  [the longest x1 467 us: on_device(): gram = lax.psum(gram_local, ('gy', 'gx'))]
    psum x1 -> x0, blocking collectives: 102 us -> none  [on_device(): sums, counts = lax.psum((local_sums, local_counts), ('gy', 'gx'))]
    all_to_all x0 -> x5, blocking collectives: none -> 66.4 us  [exchange(): return lax.all_to_all(x, axes, 0, 0)]
    ppermute x20 -> x8, starting transfers between devices: 57.7 us -> 24.3 us  [shift(): return lax.ppermute(block, axes, pairs)]
    ppermute x20 -> x8, waiting for transfers between devices: 27.2 us -> 3.59 us  [shift(): return lax.ppermute(block, axes, pairs)]
    another operation x5 -> x0, other arithmetic: 22.9 us -> none  [the longest x3 12.4 us: whitening(): lower = jnp.linalg.cholesky(gram)]
    pallas_call x0 -> x2, Pallas kernels: none -> 22.4 us  [the longest x1 15.7 us: run_finish(): pl.pallas_call(functools.partial(finish_kernel, total=total), out_shape=(...]
    dot_general x18 -> x0, matrix products: 18.4 us -> none  [the longest x8 11.1 us: one_block(): lax.dot_general(onehot, whitened, (((0,), (0,)), ((), ())), precision=hig...]
  transfers between devices with their start and end apart: 22 -> 8, of which waited for: 12 -> 1; matrix products, arithmetic and copies ran while one was open for 0% -> 1% of each run, Pallas kernels for 0% -> 0%
where the time goes in v1:
time: 127 us
  blocking collectives  73.7 us (58%)
  starting transfers between devices  24.3 us (19%)
  Pallas kernels  22.4 us (18%)
  waiting for transfers between devices  3.59 us (3%)
  local copies, waits for them, and re-layouts  1.75 us (1%)
    all_to_all x5, blocking collectives, exchange(): return lax.all_to_all(x, axes, 0, 0)  66.4 us
    ppermute x8, starting transfers between devices, shift(): return lax.ppermute(block, axes, pairs)  24.3 us
    pallas_call x1, Pallas kernels, run_finish(): pl.pallas_call(functools.partial(finish_kernel, total=total), out_shape=(...  15.7 us
    all_gather x1, blocking collectives, reduce_all(): return lax.all_gather(half, 'c', axis=0, tiled=True)  7.33 us
    pallas_call x1, Pallas kernels, run_filter(): pl.pallas_call(filter_kernel, out_shape=(jax.ShapeDtypeStruct((TH * TW, C...  6.75 us
    ppermute x8, waiting for transfers between devices, shift(): return lax.ppermute(block, axes, pairs)  3.59 us
  transfers between devices with their start and end apart: 8, of which 1 were waited for; matrix products, arithmetic and copies ran while one was open for 1% of the time, Pallas kernels for 0%

profile of v1, /device:TPU:1, one launch (start us, length us, event | category | flops | bytes accessed | tf_op | source)
XLA Modules:
  0.0 126.7 jit_solution(16978215763167014801)
XLA Ops:
  0.6 4.7 %collective-permute-start.4 = (f32[4,8,128]{2,1,0:T(8,128)}, f32[4,8,128]{2,1,0:T(8,128)S(1)}, u32[]{:S(2)}, u32[]{:S(2)}) collective-permute-start(f32[4,8,128]{2,1,0:T(8,128)} %param.4), channel_id=1, source_target_pairs={{0,32},{32,64},{64,96},{96,128},{128,160},{160,192},{192,224},{224... | collective-permute-start | bytes 49160 | tf_op jit(solution)/shard_map/ppermute | solution.py:284
  5.4 5.5 %collective-permute-start.5 = (f32[4,8,128]{2,1,0:T(8,128)}, f32[4,8,128]{2,1,0:T(8,128)S(1)}, u32[]{:S(2)}, u32[]{:S(2)}) collective-permute-start(f32[4,8,128]{2,1,0:T(8,128)} %param.4), channel_id=1, source_target_pairs={{32,0},{64,32},{96,64},{128,96},{160,128},{192,160},{224,192},{256... | collective-permute-start | bytes 49160 | tf_op jit(solution)/shard_map/ppermute | solution.py:284
  10.9 1.0 fusion.1
  11.9 1.9 %collective-permute-start.1 = (bf16[4,128,128]{2,1,0:T(8,128)(2,1)S(1)}, bf16[4,128,128]{2,1,0:T(8,128)(2,1)S(1)}, u32[]{:S(2)}, u32[]{:S(2)}) collective-permute-start(bf16[4,128,128]{2,1,0:T(8,128)(2,1)S(1)} %get-tuple-element.8), channel_id=1, source_target_pairs={{32,0},{64,32},{96,64},{128,96},{160,128},{192,160},{224,192},{256... | collective-permute-start | bytes 393224 | tf_op jit(solution)/shard_map/ppermute | solution.py:284
  13.8 3.6 %collective-permute-start = (bf16[4,128,128]{2,1,0:T(8,128)(2,1)S(1)}, bf16[4,128,128]{2,1,0:T(8,128)(2,1)S(1)}, u32[]{:S(2)}, u32[]{:S(2)}) collective-permute-start(bf16[4,128,128]{2,1,0:T(8,128)(2,1)S(1)} %get-tuple-element.9), channel_id=1, source_target_pairs={{0,32},{32,64},{64,96},{96,128},{128,160},{160,192},{192,224},{224... | collective-permute-start | bytes 393224 | tf_op jit(solution)/shard_map/ppermute | solution.py:284
  17.5 0.0 copy-start.2
  17.5 0.7 copy-done.2
  18.2 1.3 %collective-permute-start.7 = (f32[4,24,128]{2,1,0:T(8,128)S(1)}, f32[4,24,128]{2,1,0:T(8,128)S(1)}, u32[]{:S(2)}, u32[]{:S(2)}) collective-permute-start(f32[4,24,128]{2,1,0:T(8,128)S(1)} %constant_dynamic-update-slice_fusion.wc_ref), channel_id=1, source_target_pairs={{1,0},{2,1},{3,2},{4,3},{5,4},{6,5},{7,6},{8,7},{9,8},{10,9},{11,1... | collective-permute-start | bytes 147464 | tf_op jit(solution)/shard_map/ppermute | solution.py:284
  19.5 4.0 %collective-permute-start.6 = (f32[4,24,128]{2,1,0:T(8,128)S(1)}, f32[4,24,128]{2,1,0:T(8,128)S(1)}, u32[]{:S(2)}, u32[]{:S(2)}) collective-permute-start(f32[4,24,128]{2,1,0:T(8,128)S(1)} %constant_dynamic-update-slice_fusion.wc_ref), channel_id=1, source_target_pairs={{0,1},{1,2},{2,3},{3,4},{4,5},{5,6},{6,7},{7,8},{8,9},{9,10},{10,1... | collective-permute-start | bytes 147464 | tf_op jit(solution)/shard_map/ppermute | solution.py:284
  23.5 0.0 collective-permute-done.1.xs_ref
  23.6 1.9 %collective-permute-start.2 = (bf16[16,8,128]{2,1,0:T(8,128)(2,1)S(1)}, bf16[16,8,128]{2,1,0:T(8,128)(2,1)S(1)}, u32[]{:S(2)}, u32[]{:S(2)}) collective-permute-start(bf16[16,8,128]{2,1,0:T(8,128)(2,1)S(1)} %pad_maximum_fusion), channel_id=1, source_target_pairs={{0,1},{1,2},{2,3},{3,4},{4,5},{5,6},{6,7},{7,8},{8,9},{9,10},{10,1... | collective-permute-start | bytes 98312 | tf_op jit(solution)/shard_map/ppermute | solution.py:284
  25.5 0.0 copy-start.1
  25.5 1.3 %collective-permute-start.3 = (bf16[16,8,128]{2,1,0:T(8,128)(2,1)S(1)}, bf16[16,8,128]{2,1,0:T(8,128)(2,1)S(1)}, u32[]{:S(2)}, u32[]{:S(2)}) collective-permute-start(bf16[16,8,128]{2,1,0:T(8,128)(2,1)S(1)} %pad_maximum_fusion.1), channel_id=1, source_target_pairs={{1,0},{2,1},{3,2},{4,3},{5,4},{6,5},{7,6},{8,7},{9,8},{10,9},{11,1... | collective-permute-start | bytes 98312 | tf_op jit(solution)/shard_map/ppermute | solution.py:284
  26.8 0.0 collective-permute-done.7.we_ref
  26.8 0.0 collective-permute-done.2.xw_ref
  26.8 3.6 %collective-permute-done.3.xe_ref = bf16[16,8,128]{2,1,0:T(8,128)(2,1)S(1)} collective-permute-done((bf16[16,8,128]{2,1,0:T(8,128)(2,1)S(1)}, bf16[16,8,128]{2,1,0:T(8,128)(2,1)S(1)}, u32[]{:S(2)}, u32[]{:S(2)}) %collective-permute-start.3) | collective-permute-done | bytes 32800 | tf_op jit(solution)/shard_map/ppermute | solution.py:284
  30.4 6.8 %shard_map.50 = (f32[1024,128]{1,0:T(8,128)S(1)}, f32[32,40,128]{2,1,0:T(8,128)S(1)}) custom-call(bf16[8,128,128]{2,1,0:T(8,128)(2,1)S(1)} %copy-done, bf16[4,128,128]{2,1,0:T(8,128)(2,1)S(1)} %collective-permute-done.xn_ref, bf16[4,128,128]{2,1,0:T(8,128)(2,1)S(1)} %collective-permute-done.1.xs_ref, bf16[16,8,128]{2,1,0:T(8,128)(2,1)S(1)} %collective-permute-done.2.xw_ref, ...), custom_call_target="tpu_custom_call" | custom-call | tf_op jit(solution)/shard_map/pallas_call | solution.py:180
  37.2 4.3 %all_to_all.25 = f32[2,16,40,128]{3,2,1,0:T(8,128)S(1)} all-to-all(f32[2,16,40,128]{3,2,1,0:T(8,128)S(1)} %bitcast.1), channel_id=1, replica_groups=mesh['xh'=2,'y'=4,'c'=2,'zh'=4,'zl'=4,'xl'=2] {'c'}, dimensions={0} | all-to-all | bytes 1310720 | tf_op jit(solution)/shard_map/all_to_all | solution.py:288
  41.5 16.9 %all_to_all.26 = f32[16,40,128]{2,1,0:T(8,128)S(1)} all-to-all(f32[16,40,128]{2,1,0:T(8,128)S(1)} %reduce_sum.36), channel_id=1, replica_groups=mesh['xh'=2,'y'=4,'c'=2,'zh'=4,'zl'=4,'xl'=2] {'xh','y','xl'}, dimensions={0} | all-to-all | bytes 655360 | tf_op jit(solution)/shard_map/all_to_all | solution.py:288
  58.5 12.5 %all_to_all.27 = f32[4,40,128]{2,1,0:T(8,128)S(1)} all-to-all(f32[4,40,128]{2,1,0:T(8,128)S(1)} %broadcast_in_dim.6), channel_id=1, replica_groups=mesh['xh'=2,'y'=4,'c'=2,'zh'=4,'zl'=4,'xl'=2] {'zl'}, dimensions={0} | all-to-all | bytes 163840 | tf_op jit(solution)/shard_map/all_to_all | solution.py:288
  71.0 21.6 %all_to_all.28 = f32[4,40,128]{2,1,0:T(8,128)S(1)} all-to-all(f32[4,40,128]{2,1,0:T(8,128)S(1)} %broadcast_in_dim.7), channel_id=1, replica_groups=mesh['xh'=2,'y'=4,'c'=2,'zh'=4,'zl'=4,'xl'=2] {'zh'}, dimensions={0} | all-to-all | bytes 163840 | tf_op jit(solution)/shard_map/all_to_all | solution.py:288
  92.6 11.1 %all_to_all.29 = f32[16,40,128]{2,1,0:T(8,128)S(1)} all-to-all(f32[16,40,128]{2,1,0:T(8,128)S(1)} %broadcast_in_dim.8), channel_id=1, replica_groups=mesh['xh'=2,'y'=4,'c'=2,'zh'=4,'zl'=4,'xl'=2] {'xh','y','xl'}, dimensions={0} | all-to-all | bytes 655360 | tf_op jit(solution)/shard_map/all_to_all | solution.py:288
  103.7 7.3 %all_gather.3.msg_ref = f32[32,40,128]{2,1,0:T(8,128)S(1)} all-gather(f32[16,40,128]{2,1,0:T(8,128)S(1)} %all_to_all.29), channel_id=1, replica_groups=mesh['xh'=2,'y'=4,'c'=2,'zh'=4,'zl'=4,'xl'=2] {'c'}, dimensions={0}, use_global_device_ids=true | all-gather | bytes 983040 | tf_op jit(solution)/shard_map/all_gather | solution.py:301
  111.0 15.7 %shard_map.51 = (f32[8,128]{1,0:T(8,128)}, f32[1024,128]{1,0:T(8,128)}) custom-call(f32[32,40,128]{2,1,0:T(8,128)S(1)} %all_gather.3.msg_ref, f32[1024,128]{1,0:T(8,128)S(1)} %get-tuple-element.5.filt_ref), custom_call_target="tpu_custom_call" | custom-call | tf_op jit(solution)/shard_map/pallas_call | solution.py:265
  (22 shorter events, 0.2 us)
Async XLA Ops:
  0.6 16.8 %copy-start = (bf16[8,128,128]{2,1,0:T(8,128)(2,1)S(1)}, bf16[8,128,128]{2,1,0:T(8,128)(2,1)}, u32[]{:S(2)}) copy-start(bf16[8,128,128]{2,1,0:T(8,128)(2,1)} %xc_ref.1) | copy-start | bytes 786436
  0.6 16.8 %collective-permute-start.4 = (f32[4,8,128]{2,1,0:T(8,128)}, f32[4,8,128]{2,1,0:T(8,128)S(1)}, u32[]{:S(2)}, u32[]{:S(2)}) collective-permute-start(f32[4,8,128]{2,1,0:T(8,128)} %param.4), channel_id=1, source_target_pairs={{0,32},{32,64},{64,96},{96,128},{128,160},{160,192},{192,224},{224... | collective-permute-start | bytes 49160 | tf_op jit(solution)/shard_map/ppermute | solution.py:284
  5.4 12.8 %collective-permute-start.5 = (f32[4,8,128]{2,1,0:T(8,128)}, f32[4,8,128]{2,1,0:T(8,128)S(1)}, u32[]{:S(2)}, u32[]{:S(2)}) collective-permute-start(f32[4,8,128]{2,1,0:T(8,128)} %param.4), channel_id=1, source_target_pairs={{32,0},{64,32},{96,64},{128,96},{160,128},{192,160},{224,192},{256... | collective-permute-start | bytes 49160 | tf_op jit(solution)/shard_map/ppermute | solution.py:284
  11.9 11.6 %collective-permute-start.1 = (bf16[4,128,128]{2,1,0:T(8,128)(2,1)S(1)}, bf16[4,128,128]{2,1,0:T(8,128)(2,1)S(1)}, u32[]{:S(2)}, u32[]{:S(2)}) collective-permute-start(bf16[4,128,128]{2,1,0:T(8,128)(2,1)S(1)} %get-tuple-element.8), channel_id=1, source_target_pairs={{32,0},{64,32},{96,64},{128,96},{160,128},{192,160},{224,192},{256... | collective-permute-start | bytes 393224 | tf_op jit(solution)/shard_map/ppermute | solution.py:284
  13.8 9.7 %collective-permute-start = (bf16[4,128,128]{2,1,0:T(8,128)(2,1)S(1)}, bf16[4,128,128]{2,1,0:T(8,128)(2,1)S(1)}, u32[]{:S(2)}, u32[]{:S(2)}) collective-permute-start(bf16[4,128,128]{2,1,0:T(8,128)(2,1)S(1)} %get-tuple-element.9), channel_id=1, source_target_pairs={{0,32},{32,64},{64,96},{96,128},{128,160},{160,192},{192,224},{224... | collective-permute-start | bytes 393224 | tf_op jit(solution)/shard_map/ppermute | solution.py:284
  17.5 0.7 copy-start.2
  18.2 8.6 %collective-permute-start.7 = (f32[4,24,128]{2,1,0:T(8,128)S(1)}, f32[4,24,128]{2,1,0:T(8,128)S(1)}, u32[]{:S(2)}, u32[]{:S(2)}) collective-permute-start(f32[4,24,128]{2,1,0:T(8,128)S(1)} %constant_dynamic-update-slice_fusion.wc_ref), channel_id=1, source_target_pairs={{1,0},{2,1},{3,2},{4,3},{5,4},{6,5},{7,6},{8,7},{9,8},{10,9},{11,1... | collective-permute-start | bytes 147464 | tf_op jit(solution)/shard_map/ppermute | solution.py:284
  19.5 7.3 %collective-permute-start.6 = (f32[4,24,128]{2,1,0:T(8,128)S(1)}, f32[4,24,128]{2,1,0:T(8,128)S(1)}, u32[]{:S(2)}, u32[]{:S(2)}) collective-permute-start(f32[4,24,128]{2,1,0:T(8,128)S(1)} %constant_dynamic-update-slice_fusion.wc_ref), channel_id=1, source_target_pairs={{0,1},{1,2},{2,3},{3,4},{4,5},{5,6},{6,7},{7,8},{8,9},{9,10},{10,1... | collective-permute-start | bytes 147464 | tf_op jit(solution)/shard_map/ppermute | solution.py:284
  23.6 3.3 %collective-permute-start.2 = (bf16[16,8,128]{2,1,0:T(8,128)(2,1)S(1)}, bf16[16,8,128]{2,1,0:T(8,128)(2,1)S(1)}, u32[]{:S(2)}, u32[]{:S(2)}) collective-permute-start(bf16[16,8,128]{2,1,0:T(8,128)(2,1)S(1)} %pad_maximum_fusion), channel_id=1, source_target_pairs={{0,1},{1,2},{2,3},{3,4},{4,5},{5,6},{6,7},{7,8},{8,9},{9,10},{10,1... | collective-permute-start | bytes 98312 | tf_op jit(solution)/shard_map/ppermute | solution.py:284
  25.5 4.9 %copy-start.1 = (s32[8,128]{1,0:T(8,128)S(1)}, s32[8,128]{1,0:T(8,128)}, u32[]{:S(2)}) copy-start(s32[8,128]{1,0:T(8,128)} %lab_ref.1) | copy-start | bytes 12292
  25.5 4.9 %collective-permute-start.3 = (bf16[16,8,128]{2,1,0:T(8,128)(2,1)S(1)}, bf16[16,8,128]{2,1,0:T(8,128)(2,1)S(1)}, u32[]{:S(2)}, u32[]{:S(2)}) collective-permute-start(bf16[16,8,128]{2,1,0:T(8,128)(2,1)S(1)} %pad_maximum_fusion.1), channel_id=1, source_target_pairs={{1,0},{2,1},{3,2},{4,3},{5,4},{6,5},{7,6},{8,7},{9,8},{10,9},{11,1... | collective-permute-start | bytes 98312 | tf_op jit(solution)/shard_map/ppermute | solution.py:284

commit v2 on v1

--- a/solution.py
+++ b/solution.py
@@ -34,25 +34,80 @@
     return lax.dot_general(a, b, (dims, ((), ())), preferred_element_type=F32)
 
 
+ROW_PIXELS = HALO * TW
+ROW_MSG = ROW_PIXELS + 3 * 32
+COL_PIXELS = 16 * 8
+COL_MSG = COL_PIXELS + 3 * 96
+
+
+def joined(ref, first, count):
+    high, mid, low = (
+        ref[first + q * count:first + (q + 1) * count, :].astype(F32) for q in range(3)
+    )
+    return (high + mid) + low
+
+
+def pack_rows_kernel(odd_ref, x_ref, w_ref, near_ref, far_ref):
+    planes = jnp.concatenate(split3(w_ref[...].reshape(32, TW)), axis=0)
+    odd = odd_ref[0]
+    top, bottom = 0, TH - HALO
+    for ref, first in (
+        (near_ref, jnp.where(odd == 1, top, bottom)), (far_ref, jnp.where(odd == 1, bottom, top))
+    ):
+        ref[0:ROW_PIXELS, :] = x_ref[pl.ds(first, HALO)].reshape(ROW_PIXELS, C)
+        ref[ROW_PIXELS:ROW_MSG, :] = planes
+
+
+def pack_cols_kernel(odd_ref, x_ref, w_ref, row_near_ref, row_far_ref, near_ref, far_ref, wide_ref, lo_ref, hi_ref):
+    odd_row = odd_ref[0] == 1
+    near_at = jnp.where(odd_row, 0, 1)
+    for ref, at in ((row_near_ref, near_at), (row_far_ref, 1 - near_at)):
+        weights = joined(ref, ROW_PIXELS, 32)
+        for d in range(4):
+            wide_ref[d, pl.ds(pl.multiple_of(16 * at, 8), 8), :] = weights[8 * d:8 * d + 8]
+        for r in range(HALO):
+            lo_ref[12 * at + r] = ref[r * TW:r * TW + 16, :].astype(F32)[0:8]
+            hi_ref[12 * at + r] = ref[r * TW + TW - 16:r * TW + TW, :].astype(F32)[8:16]
+    for d in range(4):
+        wide_ref[d, 8:16, :] = w_ref[d]
+    for r in range(TH):
+        lo_ref[HALO + r] = x_ref[r, 0:16, :].astype(F32)[0:8]
+        hi_ref[HALO + r] = x_ref[r, TW - 16:TW, :].astype(F32)[8:16]
+    planes = jnp.concatenate(split3(wide_ref[...].reshape(96, TW)), axis=0)
+    odd_col = odd_ref[1] == 1
+    low = lo_ref[...].reshape(COL_PIXELS, C)
+    high = hi_ref[...].reshape(COL_PIXELS, C)
+    near_ref[0:COL_PIXELS, :] = jnp.where(odd_col, low, high).astype(BF16)
+    far_ref[0:COL_PIXELS, :] = jnp.where(odd_col, high, low).astype(BF16)
+    near_ref[COL_PIXELS:COL_MSG, :] = planes
+    far_ref[COL_PIXELS:COL_MSG, :] = planes
+
+
 def filter_kernel(
-    xc_ref, xn_ref, xs_ref, xw_ref, xe_ref, wc_ref, ww_ref, we_ref, lab_ref,
+    odd_ref, xc_ref, row_near_ref, row_far_ref, col_near_ref, col_far_ref, wide_ref, lab_ref,
     filt_ref, msg_ref, a_ref, b_ref, wb_ref, t_ref,
 ):
     zeros8 = jnp.zeros((16, 8, C), F32)
     for buf in (a_ref, b_ref):
         buf[:, 0:8, :] = zeros8
         buf[:, 152:160, :] = zeros8
-    a_ref[:, 8:16, :] = xw_ref[...].astype(F32)
-    a_ref[:, 144:152, :] = xe_ref[...].astype(F32)
-    a_ref[0:4, 16:144, :] = xn_ref[...].astype(F32)
+    near_at = jnp.where(odd_ref[0] == 1, 0, 1)
+    for ref, at in ((row_near_ref, near_at), (row_far_ref, 1 - near_at)):
+        a_ref[pl.ds(12 * at, HALO), 16:144, :] = ref[0:ROW_PIXELS, :].astype(F32).reshape(HALO, TW, C)
     a_ref[4:12, 16:144, :] = xc_ref[...].astype(F32)
-    a_ref[12:16, 16:144, :] = xs_ref[...].astype(F32)
-
-    lane = lax.broadcasted_iota(jnp.int32, (24, 128), 1)
+    odd_col = odd_ref[1] == 1
+    near = col_near_ref[0:COL_PIXELS, :].astype(F32).reshape(16, 8, C)
+    far = col_far_ref[0:COL_PIXELS, :].astype(F32).reshape(16, 8, C)
+    a_ref[:, 8:16, :] = jnp.where(odd_col, near, far)
+    a_ref[:, 144:152, :] = jnp.where(odd_col, far, near)
+
+    lane = lax.broadcasted_iota(jnp.int32, (96, TW), 1)
+    near = joined(col_near_ref, COL_PIXELS, 96)
+    far = joined(col_far_ref, COL_PIXELS, 96)
+    sides = jnp.where((lane < 64) != odd_col, near, far)
 
     def weights(d):
-        side = jnp.where(lane < 64, we_ref[d], ww_ref[d])
-        return jnp.concatenate([wc_ref[d], side], axis=1)
+        return jnp.concatenate([wide_ref[d], sides[24 * d:24 * d + 24]], axis=1)
 
     def right(x):
         return pltpu.roll(x, 255, 1)
@@ -176,9 +231,36 @@
             msg_ref[p, ROWS_OF + 4:BLOCK, :] = counts[0:4, lanes:lanes + TW]
 
 
-def run_filter(xc, xn, xs, xw, xe, wc, ww, we, labels):
+SCALARS = pl.BlockSpec(memory_space=pltpu.SMEM)
+VECTORS = pl.BlockSpec(memory_space=pltpu.VMEM)
+
+
+def pack_rows(odd, x, w):
+    shape = jax.ShapeDtypeStruct((ROW_MSG, C), BF16)
+    return pl.pallas_call(
+        pack_rows_kernel,
+        out_shape=(shape, shape),
+        in_specs=[SCALARS, VECTORS, VECTORS],
+        compiler_params=pltpu.CompilerParams(vmem_limit_bytes=8 * 2**20),
+    )(odd, x, w)
+
+
+def pack_cols(odd, x, w, near, far):
+    shape = jax.ShapeDtypeStruct((COL_MSG, C), BF16)
+    wide = jax.ShapeDtypeStruct((4, 24, TW), F32)
+    return pl.pallas_call(
+        pack_cols_kernel,
+        out_shape=(shape, shape, wide),
+        in_specs=[SCALARS] + [VECTORS] * 4,
+        scratch_shapes=[pltpu.VMEM((16, 8, C), F32)] * 2,
+        compiler_params=pltpu.CompilerParams(vmem_limit_bytes=8 * 2**20),
+    )(odd, x, w, near, far)
+
+
+def run_filter(*args):
     return pl.pallas_call(
         filter_kernel,
+        in_specs=[SCALARS] + [VECTORS] * 7,
         out_shape=(
             jax.ShapeDtypeStruct((TH * TW, C), F32),
             jax.ShapeDtypeStruct((PARTS, BLOCK, C), F32),
@@ -189,8 +271,51 @@
             pltpu.VMEM((4, 16, 160, C), F32),
             pltpu.VMEM((144, 128), F32),
         ],
-        compiler_params=pltpu.CompilerParams(vmem_limit_bytes=40 * 2**20),
-    )(xc, xn, xs, xw, xe, wc, ww, we, labels)
+        compiler_params=pltpu.CompilerParams(vmem_limit_bytes=32 * 2**20),
+    )(*args)
+
+
+def eliminate(g_ref, panel=64, group=8):
+    for p0 in range(0, C, panel):
+        end = p0 + panel
+        for i0 in range(p0, end, group):
+            rows = end - i0
+            left = g_ref[i0:end, 0:C]
+            right = g_ref[i0:end, C:2 * C]
+            sub = lax.broadcasted_iota(jnp.int32, (rows, C), 0)
+            cols = [jnp.broadcast_to(left[:, i0 + k:i0 + k + 1], (rows, C)) for k in range(group)]
+            lrow = [left[k:k + 1, :] for k in range(group)]
+            rrow = [right[k:k + 1, :] for k in range(group)]
+            a = [[cols[m][k:k + 1, :] for m in range(group)] for k in range(group)]
+            for k in range(group):
+                root = lax.rsqrt(a[k][k])
+                s = [a[k][m] * root for m in range(group)]
+                lrow[k] = lrow[k] * root
+                rrow[k] = rrow[k] * root
+                cols[k] = cols[k] * root
+                for m in range(k + 1, group):
+                    for n in range(m, group):
+                        a[m][n] = a[m][n] - s[m] * s[n]
+                    lrow[m] = lrow[m] - s[m] * lrow[k]
+                    rrow[m] = rrow[m] - s[m] * rrow[k]
+                    cols[m] = cols[m] - s[m] * cols[k]
+            if rows > group:
+                for k in range(group):
+                    factor = jnp.where(sub >= group, cols[k], 0.0)
+                    left = left - factor * lrow[k]
+                    right = right - factor * rrow[k]
+            for k in range(group):
+                left = jnp.where(sub == k, lrow[k], left)
+                right = jnp.where(sub == k, rrow[k], right)
+            g_ref[i0:end, 0:C] = left
+            g_ref[i0:end, C:2 * C] = right
+        if end < C:
+            uh, um, ul = split3(g_ref[p0:end, 0:C])
+            fh, fm, fl = split3(g_ref[p0:end, :])
+            lhs = jnp.concatenate([uh, um, ul, um, uh, uh], axis=0)
+            rhs = jnp.concatenate([fl, fm, fh, fh, fm, fh], axis=0)
+            update = dot(lhs, rhs, ((0,), (0,)))
+            g_ref[end:C, :] = g_ref[end:C, :] - update[end:C, :]
 
 
 def finish_kernel(msg_ref, filt_ref, best_ref, cent_ref, g_ref, *, total):
@@ -200,34 +325,7 @@
     col = lax.broadcasted_iota(jnp.int32, (C, C), 1)
     g_ref[:, C:2 * C] = jnp.where(row == col, 1.0, 0.0).astype(F32)
 
-    panel = 32
-    sub = lax.broadcasted_iota(jnp.int32, (panel, 1), 0)
-    for p0 in range(0, C, panel):
-        left = g_ref[p0:p0 + panel, 0:C]
-        right = g_ref[p0:p0 + panel, C:2 * C]
-        for i in range(panel):
-            j = p0 + i
-            column = left[:, j:j + 1]
-            pivot = left[i:i + 1, j:j + 1]
-            root = lax.rsqrt(pivot)
-            urow = left[i:i + 1, :] * root
-            irow = right[i:i + 1, :] * root
-            factor = jnp.where(sub > i, column * root, 0.0)
-            keep = sub == i
-            left = jnp.where(keep, urow, left - factor * urow)
-            right = jnp.where(keep, irow, right - factor * irow)
-        g_ref[p0:p0 + panel, 0:C] = left
-        g_ref[p0:p0 + panel, C:2 * C] = right
-        if p0 + panel < C:
-            uh, um, ul = split3(left)
-            full = jnp.concatenate([left, right], axis=1)
-            fh, fm, fl = split3(full)
-            lhs = jnp.concatenate([uh, um, ul, um, uh, uh], axis=0)
-            rhs = jnp.concatenate([fl, fm, fh, fh, fm, fh], axis=0)
-            update = dot(lhs, rhs, ((0,), (0,)))
-            rest = slice(p0 + panel, C)
-            g_ref[rest, :] = g_ref[rest, :] - update[p0 + panel:C, :]
-
+    eliminate(g_ref)
     inverse = g_ref[:, C:2 * C] * math.sqrt(total)
     ih, im, il = split3(inverse)
     lhs = jnp.concatenate([il, im, ih, im, ih, ih], axis=1)
@@ -269,7 +367,7 @@
             jax.ShapeDtypeStruct((K, C), F32),
         ),
         scratch_shapes=[pltpu.VMEM((C, 2 * C), F32)],
-        compiler_params=pltpu.CompilerParams(vmem_limit_bytes=40 * 2**20),
+        compiler_params=pltpu.CompilerParams(vmem_limit_bytes=32 * 2**20),
     )(msg, filt)
 
 
@@ -277,11 +375,12 @@
 GX = ("zh", "zl", "xl")
 
 
-def shift(block, axes, size, forward):
-    pairs = [(i, i + 1) for i in range(size - 1)]
-    if not forward:
-        pairs = [(b, a) for a, b in pairs]
-    return lax.ppermute(block, axes, pairs)
+def swap(near, far, axes, size):
+    near_pairs = [(i, i ^ 1) for i in range(size)]
+    far_pairs = [(i, i + 1) for i in range(1, size - 1, 2)]
+    far_pairs = far_pairs + [(b, a) for a, b in far_pairs]
+    far = lax.ppermute(far, axes, far_pairs)
+    return lax.ppermute(near, axes, near_pairs), far
 
 
 def exchange(x, axes):
@@ -293,8 +392,7 @@
 
 
 def reduce_all(msg):
-    msg = jnp.sum(exchange(msg.reshape(2, PARTS // 2, BLOCK, C), "c"), axis=0)
-    piece = jnp.sum(exchange(msg, ("xh", "y", "xl")), axis=0)
+    piece = jnp.sum(exchange(msg, ("c", "xh", "y", "xl")), axis=0)
     piece = jnp.sum(spread(piece, "zl", 4), axis=0)
     piece = jnp.sum(spread(piece, "zh", 4), axis=0)
     half = spread(piece, ("xh", "y", "xl"), PARTS // 2)
@@ -303,18 +401,11 @@
 
 def on_device(embeddings, affinity, assignment):
     n_gy, n_gx = 16, 32
-    xn = shift(embeddings[TH - HALO:], GY, n_gy, True)
-    xs = shift(embeddings[:HALO], GY, n_gy, False)
-    wn = shift(affinity, GY, n_gy, True)
-    ws = shift(affinity, GY, n_gy, False)
-    edge = jnp.concatenate([xn[:, TW - 8:], embeddings[:, TW - 8:], xs[:, TW - 8:]], axis=0)
-    xw = shift(edge, GX, n_gx, True)
-    edge = jnp.concatenate([xn[:, :8], embeddings[:, :8], xs[:, :8]], axis=0)
-    xe = shift(edge, GX, n_gx, False)
-    wc = jnp.concatenate([wn, affinity, ws], axis=1)
-    ww = shift(wc, GX, n_gx, True)
-    we = shift(wc, GX, n_gx, False)
-    filt, msg = run_filter(embeddings, xn, xs, xw, xe, wc, ww, we, assignment)
+    odd = jnp.stack([lax.axis_index("c"), lax.axis_index("xl")]).astype(jnp.int32)
+    rows = swap(*pack_rows(odd, embeddings, affinity), GY, n_gy)
+    near, far, wide = pack_cols(odd, embeddings, affinity, *rows)
+    cols = swap(near, far, GX, n_gx)
+    filt, msg = run_filter(odd, embeddings, *rows, *cols, wide, assignment)
     msg = reduce_all(msg)
     return run_finish(msg, filt, TH * TW * n_gy * n_gx)
 

time: 127 us -> 113 us (0.89)
  starting transfers between devices: 24.3 us -> 13.4 us
  Pallas kernels: 22.4 us -> 16.2 us
  waiting for transfers between devices: 3.59 us -> 7.46 us
    ppermute x8 -> x4, starting transfers between devices: 24.3 us -> 13.4 us  [the longest x2 10.7 us: swap(): return (lax.ppermute(near, axes, near_pairs), far)]
    pallas_call x1, Pallas kernels: 15.7 us -> 7.76 us  [run_finish(): pl.pallas_call(functools.partial(finish_kernel, total=total), out_shape=(...]
    ppermute x8 -> x4, waiting for transfers between devices: 3.59 us -> 7.46 us  [the longest x2 4.61 us: swap(): far = lax.ppermute(far, axes, far_pairs)]
    pallas_call x1 -> x3, Pallas kernels: 6.75 us -> 8.48 us  [the longest x1 7.34 us: run_filter(): pl.pallas_call(filter_kernel, in_specs=[SCALARS] + [VECTORS] * 7, out_sha...]
    all_gather x1, blocking collectives: 7.33 us -> 5.8 us  [reduce_all(): return lax.all_gather(half, 'c', axis=0, tiled=True)]
    all_to_all x5 -> x4, blocking collectives: 66.4 us -> 67.2 us  [exchange(): return lax.all_to_all(x, axes, 0, 0)]
  transfers between devices with their start and end apart: 8 -> 4, of which waited for: 1 -> 2; matrix products, arithmetic and copies ran while one was open for 1% -> 0% of each run, Pallas kernels for 0% -> 0%
where the time goes in v2:
time: 113 us
  blocking collectives  73 us (65%)
  Pallas kernels  16.2 us (14%)
  starting transfers between devices  13.4 us (12%)
  waiting for transfers between devices  7.46 us (7%)
  local copies, waits for them, and re-layouts  1.63 us (1%)
    all_to_all x4, blocking collectives, exchange(): return lax.all_to_all(x, axes, 0, 0)  67.2 us
    ppermute x2, starting transfers between devices, swap(): return (lax.ppermute(near, axes, near_pairs), far)  10.7 us
    pallas_call x1, Pallas kernels, run_finish(): pl.pallas_call(functools.partial(finish_kernel, total=total), out_shape=(...  7.76 us
    pallas_call x1, Pallas kernels, run_filter(): pl.pallas_call(filter_kernel, in_specs=[SCALARS] + [VECTORS] * 7, out_sha...  7.34 us
    all_gather x1, blocking collectives, reduce_all(): return lax.all_gather(half, 'c', axis=0, tiled=True)  5.8 us
    ppermute x2, waiting for transfers between devices, swap(): far = lax.ppermute(far, axes, far_pairs)  4.61 us
    ppermute x2, waiting for transfers between devices, swap(): return (lax.ppermute(near, axes, near_pairs), far)  2.85 us
    ppermute x2, starting transfers between devices, swap(): far = lax.ppermute(far, axes, far_pairs)  2.72 us
  transfers between devices with their start and end apart: 4, of which 2 were waited for; matrix products, arithmetic and copies ran while one was open for 0% of the time, Pallas kernels for 0%

profile of v2, /device:TPU:1, one launch (start us, length us, event | category | flops | bytes accessed | tf_op | source)
XLA Modules:
  0.0 112.7 jit_solution(15744321090757025624)
XLA Ops:
  0.6 0.1 pad_add_fusion.odd_ref
  0.7 0.6 copy-done.2
  1.4 0.9 copy-done
  2.3 0.6 shard_map.50
  2.9 8.8 %collective-permute-start = (bf16[608,128]{1,0:T(8,128)(2,1)S(1)}, bf16[608,128]{1,0:T(8,128)(2,1)S(1)}, u32[]{:S(2)}, u32[]{:S(2)}) collective-permute-start(bf16[608,128]{1,0:T(8,128)(2,1)S(1)} %get-tuple-element.9), channel_id=1, source_target_pairs={{0,32},{32,0},{64,96},{96,64},{128,160},{160,128},{192,224},{224,1... | collective-permute-start | bytes 466952 | tf_op jit(solution)/shard_map/ppermute | solution.py:383
  11.7 0.0 copy-start.1
  11.7 2.1 %collective-permute-start.1 = (bf16[608,128]{1,0:T(8,128)(2,1)S(1)}, bf16[608,128]{1,0:T(8,128)(2,1)S(1)}, u32[]{:S(2)}, u32[]{:S(2)}) collective-permute-start(bf16[608,128]{1,0:T(8,128)(2,1)S(1)} %get-tuple-element.10), channel_id=1, source_target_pairs={{32,64},{96,128},{160,192},{224,256},{288,320},{352,384},{416,448}... | collective-permute-start | bytes 466952 | tf_op jit(solution)/shard_map/ppermute | solution.py:382
  13.7 0.0 collective-permute-done.row_near_ref
  13.7 4.6 %collective-permute-done.1.row_far_ref = bf16[608,128]{1,0:T(8,128)(2,1)S(1)} collective-permute-done((bf16[608,128]{1,0:T(8,128)(2,1)S(1)}, bf16[608,128]{1,0:T(8,128)(2,1)S(1)}, u32[]{:S(2)}, u32[]{:S(2)}) %collective-permute-start.1) | collective-permute-done | bytes 155680 | tf_op jit(solution)/shard_map/ppermute | solution.py:382
  18.4 0.6 shard_map.51
  18.9 0.0 copy-start.3
  19.0 1.9 %collective-permute-start.2 = (bf16[416,128]{1,0:T(8,128)(2,1)S(1)}, bf16[416,128]{1,0:T(8,128)(2,1)S(1)}, u32[]{:S(2)}, u32[]{:S(2)}) collective-permute-start(bf16[416,128]{1,0:T(8,128)(2,1)S(1)} %get-tuple-element.11), channel_id=1, source_target_pairs={{0,1},{1,0},{2,3},{3,2},{4,5},{5,4},{6,7},{7,6},{8,9},{9,8},{10,11... | collective-permute-start | bytes 319496 | tf_op jit(solution)/shard_map/ppermute | solution.py:383
  20.9 0.7 collective-permute-start.3
  21.6 2.8 %collective-permute-done.2.col_near_ref = bf16[416,128]{1,0:T(8,128)(2,1)S(1)} collective-permute-done((bf16[416,128]{1,0:T(8,128)(2,1)S(1)}, bf16[416,128]{1,0:T(8,128)(2,1)S(1)}, u32[]{:S(2)}, u32[]{:S(2)}) %collective-permute-start.2) | collective-permute-done | bytes 106528 | tf_op jit(solution)/shard_map/ppermute | solution.py:383
  24.4 0.0 collective-permute-done.3.col_far_ref
  24.4 0.0 copy-done.3
  24.4 7.3 %shard_map.52 = (f32[1024,128]{1,0:T(8,128)S(1)}, f32[32,40,128]{2,1,0:T(8,128)S(1)}) custom-call(s32[2]{0:T(128)S(1)} %pad_add_fusion.odd_ref, bf16[8,128,128]{2,1,0:T(8,128)(2,1)S(1)} %copy-done.1, bf16[608,128]{1,0:T(8,128)(2,1)S(1)} %collective-permute-done.row_near_ref, bf16[608,128]{1,0:T(8,128)(2,1)S(1)} %collective-permute-done.1.row_far_ref, ...), custom_call_target="tpu_custom_call" | custom-call | tf_op jit(solution)/shard_map/pallas_call | solution.py:261
  31.8 19.9 %all_to_all.20 = f32[32,40,128]{2,1,0:T(8,128)S(1)} all-to-all(f32[32,40,128]{2,1,0:T(8,128)S(1)} %get-tuple-element.14), channel_id=1, replica_groups=mesh['xh'=2,'y'=4,'c'=2,'zh'=4,'zl'=4,'xl'=2] {'c','xh','y','xl'}, dimensions={0} | all-to-all | bytes 1310720 | tf_op jit(solution)/shard_map/all_to_all | solution.py:387
  51.6 0.1 reduce_sum.27
  51.7 11.4 %all_to_all.21 = f32[4,40,128]{2,1,0:T(8,128)S(1)} all-to-all(f32[4,40,128]{2,1,0:T(8,128)S(1)} %broadcast_in_dim.6), channel_id=1, replica_groups=mesh['xh'=2,'y'=4,'c'=2,'zh'=4,'zl'=4,'xl'=2] {'zl'}, dimensions={0} | all-to-all | bytes 163840 | tf_op jit(solution)/shard_map/all_to_all | solution.py:387
  63.1 24.4 %all_to_all.22 = f32[4,40,128]{2,1,0:T(8,128)S(1)} all-to-all(f32[4,40,128]{2,1,0:T(8,128)S(1)} %broadcast_in_dim.7), channel_id=1, replica_groups=mesh['xh'=2,'y'=4,'c'=2,'zh'=4,'zl'=4,'xl'=2] {'zh'}, dimensions={0} | all-to-all | bytes 163840 | tf_op jit(solution)/shard_map/all_to_all | solution.py:387
  87.5 11.6 %all_to_all.23 = f32[16,40,128]{2,1,0:T(8,128)S(1)} all-to-all(f32[16,40,128]{2,1,0:T(8,128)S(1)} %broadcast_in_dim.8), channel_id=1, replica_groups=mesh['xh'=2,'y'=4,'c'=2,'zh'=4,'zl'=4,'xl'=2] {'xh','y','xl'}, dimensions={0} | all-to-all | bytes 655360 | tf_op jit(solution)/shard_map/all_to_all | solution.py:387
  99.1 5.8 %all_gather.3.msg_ref = f32[32,40,128]{2,1,0:T(8,128)S(1)} all-gather(f32[16,40,128]{2,1,0:T(8,128)S(1)} %all_to_all.23), channel_id=1, replica_groups=mesh['xh'=2,'y'=4,'c'=2,'zh'=4,'zl'=4,'xl'=2] {'c'}, dimensions={0}, use_global_device_ids=true | all-gather | bytes 983040 | tf_op jit(solution)/shard_map/all_gather | solution.py:399
  104.9 7.8 %shard_map.53 = (f32[8,128]{1,0:T(8,128)}, f32[1024,128]{1,0:T(8,128)}) custom-call(f32[32,40,128]{2,1,0:T(8,128)S(1)} %all_gather.3.msg_ref, f32[1024,128]{1,0:T(8,128)S(1)} %get-tuple-element.15.filt_ref), custom_call_target="tpu_custom_call" | custom-call | tf_op jit(solution)/shard_map/pallas_call | solution.py:363
  (8 shorter events, 0.1 us)
Async XLA Ops:
  0.6 0.7 copy-start.2
  1.3 0.9 copy-start
  2.9 10.9 %collective-permute-start = (bf16[608,128]{1,0:T(8,128)(2,1)S(1)}, bf16[608,128]{1,0:T(8,128)(2,1)S(1)}, u32[]{:S(2)}, u32[]{:S(2)}) collective-permute-start(bf16[608,128]{1,0:T(8,128)(2,1)S(1)} %get-tuple-element.9), channel_id=1, source_target_pairs={{0,32},{32,0},{64,96},{96,64},{128,160},{160,128},{192,224},{224,1... | collective-permute-start | bytes 466952 | tf_op jit(solution)/shard_map/ppermute | solution.py:383
  11.7 12.7 %copy-start.1 = (bf16[8,128,128]{2,1,0:T(8,128)(2,1)S(1)}, bf16[8,128,128]{2,1,0:T(8,128)(2,1)}, u32[]{:S(2)}) copy-start(bf16[8,128,128]{2,1,0:T(8,128)(2,1)} %xc_ref.1) | copy-start | bytes 786436
  11.7 6.7 %collective-permute-start.1 = (bf16[608,128]{1,0:T(8,128)(2,1)S(1)}, bf16[608,128]{1,0:T(8,128)(2,1)S(1)}, u32[]{:S(2)}, u32[]{:S(2)}) collective-permute-start(bf16[608,128]{1,0:T(8,128)(2,1)S(1)} %get-tuple-element.10), channel_id=1, source_target_pairs={{32,64},{96,128},{160,192},{224,256},{288,320},{352,384},{416,448}... | collective-permute-start | bytes 466952 | tf_op jit(solution)/shard_map/ppermute | solution.py:382
  18.9 5.5 %copy-start.3 = (s32[8,128]{1,0:T(8,128)S(1)}, s32[8,128]{1,0:T(8,128)}, u32[]{:S(2)}) copy-start(s32[8,128]{1,0:T(8,128)} %lab_ref.1) | copy-start | bytes 12292
  19.0 5.4 %collective-permute-start.2 = (bf16[416,128]{1,0:T(8,128)(2,1)S(1)}, bf16[416,128]{1,0:T(8,128)(2,1)S(1)}, u32[]{:S(2)}, u32[]{:S(2)}) collective-permute-start(bf16[416,128]{1,0:T(8,128)(2,1)S(1)} %get-tuple-element.11), channel_id=1, source_target_pairs={{0,1},{1,0},{2,3},{3,2},{4,5},{5,4},{6,7},{7,6},{8,9},{9,8},{10,11... | collective-permute-start | bytes 319496 | tf_op jit(solution)/shard_map/ppermute | solution.py:383
  20.9 3.5 %collective-permute-start.3 = (bf16[416,128]{1,0:T(8,128)(2,1)S(1)}, bf16[416,128]{1,0:T(8,128)(2,1)S(1)}, u32[]{:S(2)}, u32[]{:S(2)}) collective-permute-start(bf16[416,128]{1,0:T(8,128)(2,1)S(1)} %get-tuple-element.12), channel_id=1, source_target_pairs={{1,2},{3,4},{5,6},{7,8},{9,10},{11,12},{13,14},{15,16},{17,18},{19... | collective-permute-start | bytes 319496 | tf_op jit(solution)/shard_map/ppermute | solution.py:382

commit v3 on v2

--- a/solution.py
+++ b/solution.py
@@ -14,8 +14,17 @@
 TH = 8
 TW = 128
 HALO = 4
+DEGREE = 4
 COEFFS = (0.5, 0.45, 0.35, 0.25, 0.15)
+POWERS = (
+    COEFFS[0] - COEFFS[2] + COEFFS[4],
+    COEFFS[1] - 3.0 * COEFFS[3],
+    2.0 * COEFFS[2] - 8.0 * COEFFS[4],
+    4.0 * COEFFS[3],
+    8.0 * COEFFS[4],
+)
 PARTS = 32
+HOT = 256
 BLOCK = 40
 ROWS_OF = K // PARTS
 F32 = jnp.float32
@@ -37,28 +46,52 @@
 ROW_PIXELS = HALO * TW
 ROW_MSG = ROW_PIXELS + 3 * 32
 COL_PIXELS = 16 * 8
-COL_MSG = COL_PIXELS + 3 * 96
+COL_MSG = COL_PIXELS + 3 * 8
 
 
 def joined(ref, first, count):
-    high, mid, low = (
-        ref[first + q * count:first + (q + 1) * count, :].astype(F32) for q in range(3)
+    pieces = ref[first:first + 3 * count, :].astype(F32)
+    return (pieces[0:count] + pieces[count:2 * count]) + pieces[2 * count:]
+
+
+def folded(x, first):
+    lane = lax.broadcasted_iota(jnp.int32, (8, TW), 1) // 8
+    out = jnp.zeros((8, TW), F32)
+    for v in range(12):
+        moved = pltpu.roll(x[8 * v:8 * v + 8], (8 * v - first) % TW, 1)
+        out = jnp.where(lane == v, moved, out)
+    return out
+
+
+def unfolded(low, high):
+    lane = lax.broadcasted_iota(jnp.int32, (8, TW), 1)
+    return jnp.concatenate(
+        [
+            jnp.where(
+                lane < 64,
+                pltpu.roll(low, -8 * v % TW, 1),
+                pltpu.roll(high, (TW - 8 - 8 * v) % TW, 1),
+            )
+            for v in range(12)
+        ],
+        axis=0,
     )
-    return (high + mid) + low
 
 
 def pack_rows_kernel(odd_ref, x_ref, w_ref, near_ref, far_ref):
     planes = jnp.concatenate(split3(w_ref[...].reshape(32, TW)), axis=0)
     odd = odd_ref[0]
-    top, bottom = 0, TH - HALO
-    for ref, first in (
-        (near_ref, jnp.where(odd == 1, top, bottom)), (far_ref, jnp.where(odd == 1, bottom, top))
-    ):
-        ref[0:ROW_PIXELS, :] = x_ref[pl.ds(first, HALO)].reshape(ROW_PIXELS, C)
+    for ref, first in ((near_ref, 1 - odd), (far_ref, odd)):
+        pixels = pl.ds(pl.multiple_of(first * ROW_PIXELS, ROW_PIXELS), ROW_PIXELS)
+        ref[0:ROW_PIXELS, :] = x_ref[pixels, :]
         ref[ROW_PIXELS:ROW_MSG, :] = planes
 
 
-def pack_cols_kernel(odd_ref, x_ref, w_ref, row_near_ref, row_far_ref, near_ref, far_ref, wide_ref, lo_ref, hi_ref):
+def pack_cols_kernel(
+    odd_ref, x_ref, w_ref, row_near_ref, row_far_ref,
+    near_ref, far_ref, wide_ref, x_out_ref, lo_ref, hi_ref,
+):
+    x_out_ref[...] = x_ref[...]
     odd_row = odd_ref[0] == 1
     near_at = jnp.where(odd_row, 0, 1)
     for ref, at in ((row_near_ref, near_at), (row_far_ref, 1 - near_at)):
@@ -71,41 +104,22 @@
     for d in range(4):
         wide_ref[d, 8:16, :] = w_ref[d]
     for r in range(TH):
-        lo_ref[HALO + r] = x_ref[r, 0:16, :].astype(F32)[0:8]
-        hi_ref[HALO + r] = x_ref[r, TW - 16:TW, :].astype(F32)[8:16]
-    planes = jnp.concatenate(split3(wide_ref[...].reshape(96, TW)), axis=0)
+        lo_ref[HALO + r] = x_ref[r * TW:r * TW + 16, :].astype(F32)[0:8]
+        hi_ref[HALO + r] = x_ref[r * TW + TW - 16:r * TW + TW, :].astype(F32)[8:16]
     odd_col = odd_ref[1] == 1
+    wide = wide_ref[...].reshape(96, TW)
+    low, high = folded(wide, 0), folded(wide, TW - 8)
+    for ref, part in (
+        (near_ref, jnp.where(odd_col, low, high)), (far_ref, jnp.where(odd_col, high, low))
+    ):
+        ref[COL_PIXELS:COL_MSG, :] = jnp.concatenate([q.astype(F32) for q in split3(part)], axis=0).astype(BF16)
     low = lo_ref[...].reshape(COL_PIXELS, C)
     high = hi_ref[...].reshape(COL_PIXELS, C)
     near_ref[0:COL_PIXELS, :] = jnp.where(odd_col, low, high).astype(BF16)
     far_ref[0:COL_PIXELS, :] = jnp.where(odd_col, high, low).astype(BF16)
-    near_ref[COL_PIXELS:COL_MSG, :] = planes
-    far_ref[COL_PIXELS:COL_MSG, :] = planes
-
-
-def filter_kernel(
-    odd_ref, xc_ref, row_near_ref, row_far_ref, col_near_ref, col_far_ref, wide_ref, lab_ref,
-    filt_ref, msg_ref, a_ref, b_ref, wb_ref, t_ref,
-):
-    zeros8 = jnp.zeros((16, 8, C), F32)
-    for buf in (a_ref, b_ref):
-        buf[:, 0:8, :] = zeros8
-        buf[:, 152:160, :] = zeros8
-    near_at = jnp.where(odd_ref[0] == 1, 0, 1)
-    for ref, at in ((row_near_ref, near_at), (row_far_ref, 1 - near_at)):
-        a_ref[pl.ds(12 * at, HALO), 16:144, :] = ref[0:ROW_PIXELS, :].astype(F32).reshape(HALO, TW, C)
-    a_ref[4:12, 16:144, :] = xc_ref[...].astype(F32)
-    odd_col = odd_ref[1] == 1
-    near = col_near_ref[0:COL_PIXELS, :].astype(F32).reshape(16, 8, C)
-    far = col_far_ref[0:COL_PIXELS, :].astype(F32).reshape(16, 8, C)
-    a_ref[:, 8:16, :] = jnp.where(odd_col, near, far)
-    a_ref[:, 144:152, :] = jnp.where(odd_col, far, near)
-
-    lane = lax.broadcasted_iota(jnp.int32, (96, TW), 1)
-    near = joined(col_near_ref, COL_PIXELS, 96)
-    far = joined(col_far_ref, COL_PIXELS, 96)
-    sides = jnp.where((lane < 64) != odd_col, near, far)
-
+
+
+def normed_weights(wide_ref, sides):
     def weights(d):
         return jnp.concatenate([wide_ref[d], sides[24 * d:24 * d + 24]], axis=1)
 
@@ -134,74 +148,109 @@
         scale * diag * right(below),
         scale * anti * left(below),
     )
-    stack = jnp.concatenate(normed + (jnp.zeros((32, 256), F32),), axis=0)
-    centre = stack[:, 0:128].T
-    sides = stack[:, 128:256].T
-    t_ref[0:8, :] = sides[120:128]
-    t_ref[8:136, :] = centre
-    t_ref[136:144, :] = sides[0:8]
+    return jnp.concatenate(normed + (jnp.zeros((32, 256), F32),), axis=0)
+
+
+def spread_weights(wb_ref, columns, first):
+    count = columns.shape[0]
     for d in range(4):
         for r in range(16):
             k = d * 24 + r + 4
-            wb_ref[d, r, 0:8, :] = jnp.zeros((8, C), F32)
-            wb_ref[d, r, 152:160, :] = jnp.zeros((8, C), F32)
-            wb_ref[d, r, 8:152, :] = jnp.broadcast_to(t_ref[:, k:k + 1], (144, C))
-
-    def apply_at(src, r, s, n):
-        here, before, after = pl.ds(s, n), pl.ds(s - 1, n), pl.ds(s + 1, n)
-        out = wb_ref[0, r, here, :] * src[r, after, :]
-        out = out + wb_ref[0, r, before, :] * src[r, before, :]
-        out = out + wb_ref[1, r, here, :] * src[r + 1, here, :]
-        out = out + wb_ref[1, r - 1, here, :] * src[r - 1, here, :]
-        out = out + wb_ref[2, r, here, :] * src[r + 1, after, :]
-        out = out + wb_ref[2, r - 1, before, :] * src[r - 1, before, :]
-        out = out + wb_ref[3, r, here, :] * src[r + 1, before, :]
-        return out + wb_ref[3, r - 1, after, :] * src[r - 1, after, :]
-
-    step = 24
-
-    def first(r, carry):
-        for s in range(8, 152, step):
-            b_ref[r, s:s + step, :] = apply_at(a_ref, r, s, step)
-        return carry
-
-    def later(cur, prev):
-        def body(r, carry):
-            for s in range(8, 152, step):
-                new = 2.0 * apply_at(cur, r, s, step) - prev[r, s:s + step, :]
-                prev[r, s:s + step, :] = new
-            return carry
-        return body
-
-    def accumulate(r, carry):
-        for s in range(0, TW, 32):
-            total = COEFFS[0] * a_ref[r + 4, 16 + s:48 + s, :] + COEFFS[1] * b_ref[r + 4, 16 + s:48 + s, :]
-            filt_ref[pl.ds(r * TW + s, 32), :] = total
-        return carry
-
-    def add(src, coeff):
-        def body(r, carry):
-            for s in range(0, TW, 32):
-                rows = pl.ds(r * TW + s, 32)
-                filt_ref[rows, :] = filt_ref[rows, :] + coeff * src[r + 4, 16 + s:48 + s, :]
-            return carry
-        return body
-
-    def last(r, carry):
-        for s in range(0, TW, 16):
-            here = pl.ds(s + 16, 16)
-            new = 2.0 * apply_at(b_ref, r + 4, s + 16, 16) - a_ref[r + 4, here, :]
-            rows = pl.ds(r * TW + s, 16)
-            filt_ref[rows, :] = filt_ref[rows, :] + COEFFS[4] * new
-        return carry
-
-    lax.fori_loop(1, 15, first, 0)
-    lax.fori_loop(0, TH, accumulate, 0)
-    lax.fori_loop(2, 14, later(b_ref, a_ref), 0)
-    lax.fori_loop(0, TH, add(a_ref, COEFFS[2]), 0)
-    lax.fori_loop(3, 13, later(a_ref, b_ref), 0)
-    lax.fori_loop(0, TH, add(b_ref, COEFFS[3]), 0)
-    lax.fori_loop(0, TH, last, 0)
+            wb_ref[d, r, first:first + count, :] = jnp.broadcast_to(columns[:, k:k + 1], (count, C))
+
+
+def apply_rows(wb_ref, src, r, rows, s):
+    x, w = {}, {}
+
+    def field(q, off):
+        if (q, off) not in x:
+            x[q, off] = src[r + q, s + off:s + off + 8, :]
+        return x[q, off]
+
+    def weight(d, q, off):
+        if (d, q, off) not in w:
+            w[d, q, off] = wb_ref[d, r + q, s + off:s + off + 8, :]
+        return w[d, q, off]
+
+    outs = []
+    for q in range(rows):
+        out = weight(0, q, 0) * field(q, 1) + weight(0, q, -1) * field(q, -1)
+        out = out + weight(1, q - 1, 0) * field(q - 1, 0)
+        out = out + weight(2, q - 1, -1) * field(q - 1, -1)
+        out = out + weight(3, q - 1, 1) * field(q - 1, 1)
+        out = out + weight(1, q, 0) * field(q + 1, 0)
+        out = out + weight(2, q, 0) * field(q + 1, 1)
+        outs.append(out + weight(3, q, 0) * field(q + 1, -1))
+    return outs
+
+
+def sweep(step, tiles, wb_ref, start_ref, src, dst):
+    rows = (16 - 2 * step) // 2
+    for r in (step, step + rows):
+        for t in tiles:
+            s = 8 + 8 * t
+            for q, new in enumerate(apply_rows(wb_ref, src, r, rows, s)):
+                start = start_ref[r + q, s:s + 8, :]
+                if step == 1:
+                    new = POWERS[4] * new + POWERS[3] * start
+                else:
+                    new = new + POWERS[DEGREE - step] * start
+                if step < DEGREE:
+                    dst[r + q, s:s + 8, :] = new
+                else:
+                    pixel = (r + q - 4) * TW + s - 16
+                    dst[pixel:pixel + 8, :] = new
+
+
+def prepare_kernel(
+    odd_ref, x_ref, row_near_ref, row_far_ref, wide_ref, lab_ref,
+    hot_ref, count_ref, a_ref, b_ref, c_ref, filt_ref, wb_ref,
+):
+    zeros8 = jnp.zeros((16, 8, C), F32)
+    for buf in (a_ref, b_ref, c_ref, wb_ref.at[0], wb_ref.at[1], wb_ref.at[2], wb_ref.at[3]):
+        buf[:, 0:8, :] = zeros8
+        buf[:, 152:160, :] = zeros8
+    near_at = jnp.where(odd_ref[0] == 1, 0, 1)
+    for ref, at in ((row_near_ref, near_at), (row_far_ref, 1 - near_at)):
+        a_ref[pl.ds(12 * at, HALO), 16:144, :] = ref[0:ROW_PIXELS, :].astype(F32).reshape(HALO, TW, C)
+    a_ref[4:12, 16:144, :] = x_ref[...].astype(F32).reshape(TH, TW, C)
+    stack = normed_weights(wide_ref, jnp.zeros((96, TW), F32))
+    spread_weights(wb_ref, stack[:, 0:TW].T[8:120], 24)
+    sweep(1, range(3, 15), wb_ref, a_ref, a_ref, b_ref)
+    sweep(2, range(4, 14), wb_ref, a_ref, b_ref, c_ref)
+    sweep(3, range(5, 13), wb_ref, a_ref, c_ref, b_ref)
+    sweep(4, range(6, 12), wb_ref, a_ref, b_ref, filt_ref)
+    ones = jnp.ones((8, TH * TW), BF16)
+    for k0 in range(0, K, HOT):
+        cluster = lax.broadcasted_iota(jnp.int32, (HOT, TW), 0) + k0
+        onehot = jnp.concatenate(
+            [(cluster == lab_ref[r:r + 1, :]).astype(F32).astype(BF16) for r in range(TH)], axis=1
+        )
+        hot_ref[k0:k0 + HOT, :] = onehot
+        count_ref[:, k0:k0 + HOT] = dot(ones, onehot, ((1,), (1,)))
+
+
+def filter_kernel(
+    odd_ref, col_near_ref, col_far_ref, wide_ref, hot_ref, count_ref, *refs,
+):
+    a_ref, b_ref, c_ref, filt_ref, wb_ref, msg_ref = refs[5:]
+    odd_col = odd_ref[1] == 1
+    near = col_near_ref[0:COL_PIXELS, :].astype(F32).reshape(16, 8, C)
+    far = col_far_ref[0:COL_PIXELS, :].astype(F32).reshape(16, 8, C)
+    a_ref[:, 8:16, :] = jnp.where(odd_col, near, far)
+    a_ref[:, 144:152, :] = jnp.where(odd_col, far, near)
+    near = joined(col_near_ref, COL_PIXELS, 8)
+    far = joined(col_far_ref, COL_PIXELS, 8)
+    sides = unfolded(jnp.where(odd_col, far, near), jnp.where(odd_col, near, far))
+    stack = normed_weights(wide_ref, sides)
+    centre = stack[:, 0:TW].T
+    sides = stack[:, TW:2 * TW].T
+    spread_weights(wb_ref, jnp.concatenate([sides[120:128], centre[0:8]], axis=0), 8)
+    spread_weights(wb_ref, jnp.concatenate([centre[120:128], sides[0:8]], axis=0), 136)
+    sweep(1, (0, 1, 2, 15, 16, 17), wb_ref, a_ref, a_ref, b_ref)
+    sweep(2, (0, 1, 2, 3, 14, 15, 16, 17), wb_ref, a_ref, b_ref, c_ref)
+    sweep(3, (0, 1, 2, 3, 4, 13, 14, 15, 16, 17), wb_ref, a_ref, c_ref, b_ref)
+    sweep(4, (1, 2, 3, 4, 5, 12, 13, 14, 15, 16), wb_ref, a_ref, b_ref, filt_ref)
 
     high, mid, low = split3(filt_ref[...])
     tall = ((0,), (0,))
@@ -213,22 +262,15 @@
     gram = gram + by_high[:, :C]
 
     pieces = jnp.concatenate([high, mid, low], axis=1)
-    ones = jnp.ones((8, TH * TW), BF16)
-    chunk = 256
-    for k0 in range(0, K, chunk):
-        cluster = lax.broadcasted_iota(jnp.int32, (chunk, TW), 0) + k0
-        onehot = jnp.concatenate(
-            [(cluster == lab_ref[r:r + 1, :]).astype(F32).astype(BF16) for r in range(TH)], axis=1
-        )
-        part = dot(onehot, pieces, ((1,), (0,)))
+    for k0 in range(0, K, HOT):
+        part = dot(hot_ref[k0:k0 + HOT, :], pieces, ((1,), (0,)))
         part = (part[:, 2 * C:] + part[:, C:2 * C]) + part[:, :C]
-        counts = dot(ones, onehot, ((1,), (1,)))
-        for q in range(chunk // ROWS_OF):
+        for q in range(HOT // ROWS_OF):
             p = k0 // ROWS_OF + q
             msg_ref[p, 0:ROWS_OF, :] = part[q * ROWS_OF:(q + 1) * ROWS_OF]
             msg_ref[p, ROWS_OF:ROWS_OF + 4, :] = gram[4 * p:4 * p + 4]
-            lanes = (p * ROWS_OF - k0) // TW * TW
-            msg_ref[p, ROWS_OF + 4:BLOCK, :] = counts[0:4, lanes:lanes + TW]
+            lanes = p * ROWS_OF // TW * TW
+            msg_ref[p, ROWS_OF + 4:BLOCK, :] = count_ref[0:4, lanes:lanes + TW]
 
 
 SCALARS = pl.BlockSpec(memory_space=pltpu.SMEM)
@@ -240,39 +282,64 @@
     return pl.pallas_call(
         pack_rows_kernel,
         out_shape=(shape, shape),
-        in_specs=[SCALARS, VECTORS, VECTORS],
+        in_specs=[SCALARS] + [VECTORS] * 2,
+        out_specs=(VECTORS,) * 2,
         compiler_params=pltpu.CompilerParams(vmem_limit_bytes=8 * 2**20),
-    )(odd, x, w)
+    )(odd, x.reshape(TH * TW, C), w)
 
 
 def pack_cols(odd, x, w, near, far):
     shape = jax.ShapeDtypeStruct((COL_MSG, C), BF16)
-    wide = jax.ShapeDtypeStruct((4, 24, TW), F32)
     return pl.pallas_call(
         pack_cols_kernel,
-        out_shape=(shape, shape, wide),
+        out_shape=(
+            shape,
+            shape,
+            jax.ShapeDtypeStruct((4, 24, TW), F32),
+            jax.ShapeDtypeStruct((TH * TW, C), BF16),
+        ),
         in_specs=[SCALARS] + [VECTORS] * 4,
+        out_specs=(VECTORS,) * 4,
         scratch_shapes=[pltpu.VMEM((16, 8, C), F32)] * 2,
         compiler_params=pltpu.CompilerParams(vmem_limit_bytes=8 * 2**20),
-    )(odd, x, w, near, far)
-
-
-def run_filter(*args):
+    )(odd, x.reshape(TH * TW, C), w, near, far)
+
+
+FIELD = jax.ShapeDtypeStruct((16, 160, C), F32)
+BUFFERS = (
+    FIELD,
+    FIELD,
+    FIELD,
+    jax.ShapeDtypeStruct((TH * TW, C), F32),
+    jax.ShapeDtypeStruct((4, 16, 160, C), F32),
+)
+
+
+def run_prepare(odd, x, near, far, wide, labels):
+    outs = (
+        jax.ShapeDtypeStruct((K, TH * TW), BF16),
+        jax.ShapeDtypeStruct((8, K), F32),
+    ) + BUFFERS
     return pl.pallas_call(
+        prepare_kernel,
+        out_shape=outs,
+        in_specs=[SCALARS] + [VECTORS] * 5,
+        out_specs=(VECTORS,) * 7,
+        compiler_params=pltpu.CompilerParams(vmem_limit_bytes=16 * 2**20),
+        cost_estimate=pl.CostEstimate(flops=2**27, bytes_accessed=2**23, transcendentals=0),
+    )(odd, x, near, far, wide, labels)
+
+
+def run_filter(odd, near, far, wide, hot, counts, *buffers):
+    *_, filt, _, msg = pl.pallas_call(
         filter_kernel,
-        in_specs=[SCALARS] + [VECTORS] * 7,
-        out_shape=(
-            jax.ShapeDtypeStruct((TH * TW, C), F32),
-            jax.ShapeDtypeStruct((PARTS, BLOCK, C), F32),
-        ),
-        scratch_shapes=[
-            pltpu.VMEM((16, 160, C), F32),
-            pltpu.VMEM((16, 160, C), F32),
-            pltpu.VMEM((4, 16, 160, C), F32),
-            pltpu.VMEM((144, 128), F32),
-        ],
-        compiler_params=pltpu.CompilerParams(vmem_limit_bytes=32 * 2**20),
-    )(*args)
+        in_specs=[SCALARS] + [VECTORS] * 10,
+        out_shape=BUFFERS + (jax.ShapeDtypeStruct((PARTS, BLOCK, C), F32),),
+        out_specs=(VECTORS,) * 6,
+        input_output_aliases={6 + q: q for q in range(5)},
+        compiler_params=pltpu.CompilerParams(vmem_limit_bytes=16 * 2**20),
+    )(odd, near, far, wide, hot, counts, *buffers)
+    return filt, msg
 
 
 def eliminate(g_ref, panel=64, group=8):
@@ -403,9 +470,10 @@
     n_gy, n_gx = 16, 32
     odd = jnp.stack([lax.axis_index("c"), lax.axis_index("xl")]).astype(jnp.int32)
     rows = swap(*pack_rows(odd, embeddings, affinity), GY, n_gy)
-    near, far, wide = pack_cols(odd, embeddings, affinity, *rows)
+    near, far, wide, pixels = pack_cols(odd, embeddings, affinity, *rows)
+    prepared = run_prepare(odd, pixels, *rows, wide, assignment)
     cols = swap(near, far, GX, n_gx)
-    filt, msg = run_filter(odd, embeddings, *rows, *cols, wide, assignment)
+    filt, msg = run_filter(odd, *cols, wide, *prepared)
     msg = reduce_all(msg)
     return run_finish(msg, filt, TH * TW * n_gy * n_gx)
 

time: 113 us -> 110 us (0.973)
  waiting for transfers between devices: 7.46 us -> 4.62 us
  blocking collectives: 73 us -> 71.4 us
    ppermute x2, waiting for transfers between devices: 2.85 us -> 0.01 us  [swap(): return (lax.ppermute(near, axes, near_pairs), far)]
    all_to_all x4, blocking collectives: 67.2 us -> 65 us  [exchange(): return lax.all_to_all(x, axes, 0, 0)]
    pallas_call x2 -> x3, Pallas kernels: 7.91 us -> 8.75 us  [the longest x1 4.36 us: run_filter(): pl.pallas_call(filter_kernel, in_specs=[SCALARS] + [VECTORS] * 10, out_sh...]
    unnamed x8 -> x6, local copies, waits for them, and re-layouts: 1.59 us -> 2.35 us
  transfers between devices with their start and end apart: 4 -> 4, of which waited for: 2 -> 1; matrix products, arithmetic and copies ran while one was open for 0% -> 0% of each run, Pallas kernels for 0% -> 3%
where the time goes in v3:
time: 110 us
  blocking collectives  71.4 us (65%)
  Pallas kernels  17.1 us (16%)
  starting transfers between devices  13.3 us (12%)
  waiting for transfers between devices  4.62 us (4%)
  local copies, waits for them, and re-layouts  2.39 us (2%)
    all_to_all x4, blocking collectives, exchange(): return lax.all_to_all(x, axes, 0, 0)  65 us
    ppermute x2, starting transfers between devices, swap(): return (lax.ppermute(near, axes, near_pairs), far)  10.7 us
    pallas_call x1, Pallas kernels, run_finish(): pl.pallas_call(functools.partial(finish_kernel, total=total), out_shape=(...  7.76 us
    all_gather x1, blocking collectives, reduce_all(): return lax.all_gather(half, 'c', axis=0, tiled=True)  6.45 us
    ppermute x2, waiting for transfers between devices, swap(): far = lax.ppermute(far, axes, far_pairs)  4.61 us
    pallas_call x1, Pallas kernels, run_filter(): pl.pallas_call(filter_kernel, in_specs=[SCALARS] + [VECTORS] * 10, out_sh...  4.36 us
    pallas_call x1, Pallas kernels, run_prepare(): pl.pallas_call(prepare_kernel, out_shape=outs, in_specs=[SCALARS] + [VECT...  3.73 us
    ppermute x2, starting transfers between devices, swap(): far = lax.ppermute(far, axes, far_pairs)  2.58 us
  transfers between devices with their start and end apart: 4, of which 1 were waited for; matrix products, arithmetic and copies ran while one was open for 0% of the time, Pallas kernels for 3%

profile of v3, /device:TPU:1, one launch (start us, length us, event | category | flops | bytes accessed | tf_op | source)
XLA Modules:
  0.0 109.7 jit_solution(5589488020906068461)
XLA Ops:
  0.6 0.1 pad_add_fusion.odd_ref
  0.7 0.9 copy-done
  1.7 0.7 copy-done.1
  2.4 0.6 shard_map.50
  2.9 8.8 %collective-permute-start = (bf16[608,128]{1,0:T(8,128)(2,1)S(1)}, bf16[608,128]{1,0:T(8,128)(2,1)S(1)}, u32[]{:S(2)}, u32[]{:S(2)}) collective-permute-start(bf16[608,128]{1,0:T(8,128)(2,1)S(1)} %get-tuple-element.17), channel_id=1, source_target_pairs={{0,32},{32,0},{64,96},{96,64},{128,160},{160,128},{192,224},{224,1... | collective-permute-start | bytes 466952 | tf_op jit(solution)/shard_map/ppermute | solution.py:450
  11.7 1.9 %collective-permute-start.1 = (bf16[608,128]{1,0:T(8,128)(2,1)S(1)}, bf16[608,128]{1,0:T(8,128)(2,1)S(1)}, u32[]{:S(2)}, u32[]{:S(2)}) collective-permute-start(bf16[608,128]{1,0:T(8,128)(2,1)S(1)} %get-tuple-element.18), channel_id=1, source_target_pairs={{32,64},{96,128},{160,192},{224,256},{288,320},{352,384},{416,448}... | collective-permute-start | bytes 466952 | tf_op jit(solution)/shard_map/ppermute | solution.py:449
  13.7 0.0 collective-permute-done.row_near_ref
  13.7 4.6 %collective-permute-done.1.row_far_ref = bf16[608,128]{1,0:T(8,128)(2,1)S(1)} collective-permute-done((bf16[608,128]{1,0:T(8,128)(2,1)S(1)}, bf16[608,128]{1,0:T(8,128)(2,1)S(1)}, u32[]{:S(2)}, u32[]{:S(2)}) %collective-permute-start.1) | collective-permute-done | bytes 155680 | tf_op jit(solution)/shard_map/ppermute | solution.py:449
  18.3 0.7 shard_map.51
  19.0 1.9 %collective-permute-start.2 = (bf16[152,128]{1,0:T(8,128)(2,1)S(1)}, bf16[152,128]{1,0:T(8,128)(2,1)S(1)}, u32[]{:S(2)}, u32[]{:S(2)}) collective-permute-start(bf16[152,128]{1,0:T(8,128)(2,1)S(1)} %get-tuple-element.19), channel_id=1, source_target_pairs={{0,1},{1,0},{2,3},{3,2},{4,5},{5,4},{6,7},{7,6},{8,9},{9,8},{10,11... | collective-permute-start | bytes 116744 | tf_op jit(solution)/shard_map/ppermute | solution.py:450
  20.9 0.7 collective-permute-start.3
  21.6 0.0 copy-start.2
  21.6 0.7 copy-done.2
  22.2 3.7 %shard_map.52 = (bf16[1024,1024]{1,0:T(8,128)(2,1)S(1)}, f32[8,1024]{1,0:T(8,128)S(1)}, f32[16,160,128]{2,1,0:T(8,128)S(1)}, f32[16,160,128]{2,1,0:T(8,128)S(1)}...) custom-call(s32[2]{0:T(128)S(1)} %pad_add_fusion.odd_ref, ...), custom_call_target="tpu_custom_call" | custom-call | flops 134217728 | bytes 8388608 | tf_op jit(solution)/shard_map/pallas_call | solution.py:323
  26.0 0.0 collective-permute-done.2.col_near_ref
  26.0 0.0 collective-permute-done.3.col_far_ref
  26.0 4.4 %shard_map.53 = (f32[16,160,128]{2,1,0:T(8,128)S(1)}, f32[16,160,128]{2,1,0:T(8,128)S(1)}, f32[16,160,128]{2,1,0:T(8,128)S(1)}, f32[1024,128]{1,0:T(8,128)S(1)},...) custom-call(s32[2]{0:T(128)S(1)} %pad_add_fusion.odd_ref, ...), custom_call_target="tpu_custom_call", output_to_operand_aliasing={{0}: (6, {}), {1}: (7, {}), {2}: (8, {}), {3}: (9, {}), {4}... | custom-call | tf_op jit(solution)/shard_map/pallas_call | solution.py:334
  30.4 20.4 %all_to_all.20 = f32[32,40,128]{2,1,0:T(8,128)S(1)} all-to-all(f32[32,40,128]{2,1,0:T(8,128)S(1)} %get-tuple-element.30), channel_id=1, replica_groups=mesh['xh'=2,'y'=4,'c'=2,'zh'=4,'zl'=4,'xl'=2] {'c','xh','y','xl'}, dimensions={0} | all-to-all | bytes 1310720 | tf_op jit(solution)/shard_map/all_to_all | solution.py:454
  50.8 0.1 reduce_sum.27
  50.8 11.4 %all_to_all.21 = f32[4,40,128]{2,1,0:T(8,128)S(1)} all-to-all(f32[4,40,128]{2,1,0:T(8,128)S(1)} %broadcast_in_dim.6), channel_id=1, replica_groups=mesh['xh'=2,'y'=4,'c'=2,'zh'=4,'zl'=4,'xl'=2] {'zl'}, dimensions={0} | all-to-all | bytes 163840 | tf_op jit(solution)/shard_map/all_to_all | solution.py:454
  62.3 22.7 %all_to_all.22 = f32[4,40,128]{2,1,0:T(8,128)S(1)} all-to-all(f32[4,40,128]{2,1,0:T(8,128)S(1)} %broadcast_in_dim.7), channel_id=1, replica_groups=mesh['xh'=2,'y'=4,'c'=2,'zh'=4,'zl'=4,'xl'=2] {'zh'}, dimensions={0} | all-to-all | bytes 163840 | tf_op jit(solution)/shard_map/all_to_all | solution.py:454
  85.0 10.5 %all_to_all.23 = f32[16,40,128]{2,1,0:T(8,128)S(1)} all-to-all(f32[16,40,128]{2,1,0:T(8,128)S(1)} %broadcast_in_dim.8), channel_id=1, replica_groups=mesh['xh'=2,'y'=4,'c'=2,'zh'=4,'zl'=4,'xl'=2] {'xh','y','xl'}, dimensions={0} | all-to-all | bytes 655360 | tf_op jit(solution)/shard_map/all_to_all | solution.py:454
  95.5 6.5 %all_gather.3.msg_ref = f32[32,40,128]{2,1,0:T(8,128)S(1)} all-gather(f32[16,40,128]{2,1,0:T(8,128)S(1)} %all_to_all.23), channel_id=1, replica_groups=mesh['xh'=2,'y'=4,'c'=2,'zh'=4,'zl'=4,'xl'=2] {'c'}, dimensions={0}, use_global_device_ids=true | all-gather | bytes 983040 | tf_op jit(solution)/shard_map/all_gather | solution.py:466
  101.9 7.8 %shard_map.54 = (f32[8,128]{1,0:T(8,128)}, f32[1024,128]{1,0:T(8,128)}) custom-call(f32[32,40,128]{2,1,0:T(8,128)S(1)} %all_gather.3.msg_ref, f32[1024,128]{1,0:T(8,128)S(1)} %get-tuple-element.31.filt_ref), custom_call_target="tpu_custom_call" | custom-call | tf_op jit(solution)/shard_map/pallas_call | solution.py:430
  (7 shorter events, 0.1 us)
Async XLA Ops:
  0.7 1.0 copy-start
  1.7 0.7 copy-start.1
  2.9 10.7 %collective-permute-start = (bf16[608,128]{1,0:T(8,128)(2,1)S(1)}, bf16[608,128]{1,0:T(8,128)(2,1)S(1)}, u32[]{:S(2)}, u32[]{:S(2)}) collective-permute-start(bf16[608,128]{1,0:T(8,128)(2,1)S(1)} %get-tuple-element.17), channel_id=1, source_target_pairs={{0,32},{32,0},{64,96},{96,64},{128,160},{160,128},{192,224},{224,1... | collective-permute-start | bytes 466952 | tf_op jit(solution)/shard_map/ppermute | solution.py:450
  11.7 6.5 %collective-permute-start.1 = (bf16[608,128]{1,0:T(8,128)(2,1)S(1)}, bf16[608,128]{1,0:T(8,128)(2,1)S(1)}, u32[]{:S(2)}, u32[]{:S(2)}) collective-permute-start(bf16[608,128]{1,0:T(8,128)(2,1)S(1)} %get-tuple-element.18), channel_id=1, source_target_pairs={{32,64},{96,128},{160,192},{224,256},{288,320},{352,384},{416,448}... | collective-permute-start | bytes 466952 | tf_op jit(solution)/shard_map/ppermute | solution.py:449
  19.0 7.0 %collective-permute-start.2 = (bf16[152,128]{1,0:T(8,128)(2,1)S(1)}, bf16[152,128]{1,0:T(8,128)(2,1)S(1)}, u32[]{:S(2)}, u32[]{:S(2)}) collective-permute-start(bf16[152,128]{1,0:T(8,128)(2,1)S(1)} %get-tuple-element.19), channel_id=1, source_target_pairs={{0,1},{1,0},{2,3},{3,2},{4,5},{5,4},{6,7},{7,6},{8,9},{9,8},{10,11... | collective-permute-start | bytes 116744 | tf_op jit(solution)/shard_map/ppermute | solution.py:450
  20.9 5.1 %collective-permute-start.3 = (bf16[152,128]{1,0:T(8,128)(2,1)S(1)}, bf16[152,128]{1,0:T(8,128)(2,1)S(1)}, u32[]{:S(2)}, u32[]{:S(2)}) collective-permute-start(bf16[152,128]{1,0:T(8,128)(2,1)S(1)} %get-tuple-element.20), channel_id=1, source_target_pairs={{1,2},{3,4},{5,6},{7,8},{9,10},{11,12},{13,14},{15,16},{17,18},{19... | collective-permute-start | bytes 116744 | tf_op jit(solution)/shard_map/ppermute | solution.py:449
  21.6 0.7 copy-start.2

commit v4 on v3

--- a/solution.py
+++ b/solution.py
@@ -262,15 +262,13 @@
     gram = gram + by_high[:, :C]
 
     pieces = jnp.concatenate([high, mid, low], axis=1)
-    for k0 in range(0, K, HOT):
-        part = dot(hot_ref[k0:k0 + HOT, :], pieces, ((1,), (0,)))
-        part = (part[:, 2 * C:] + part[:, C:2 * C]) + part[:, :C]
-        for q in range(HOT // ROWS_OF):
-            p = k0 // ROWS_OF + q
-            msg_ref[p, 0:ROWS_OF, :] = part[q * ROWS_OF:(q + 1) * ROWS_OF]
-            msg_ref[p, ROWS_OF:ROWS_OF + 4, :] = gram[4 * p:4 * p + 4]
-            lanes = p * ROWS_OF // TW * TW
-            msg_ref[p, ROWS_OF + 4:BLOCK, :] = count_ref[0:4, lanes:lanes + TW]
+    part = dot(hot_ref[...], pieces, ((1,), (0,)))
+    part = (part[:, 2 * C:] + part[:, C:2 * C]) + part[:, :C]
+    msg_ref[:, 0:ROWS_OF, :] = part.reshape(PARTS, ROWS_OF, C)
+    msg_ref[:, ROWS_OF:ROWS_OF + 4, :] = gram.reshape(PARTS, 4, C)
+    for p in range(PARTS):
+        lanes = p * ROWS_OF // TW * TW
+        msg_ref[p, ROWS_OF + 4:BLOCK, :] = count_ref[0:4, lanes:lanes + TW]
 
 
 SCALARS = pl.BlockSpec(memory_space=pltpu.SMEM)
@@ -385,7 +383,7 @@
             g_ref[end:C, :] = g_ref[end:C, :] - update[end:C, :]
 
 
-def finish_kernel(msg_ref, filt_ref, best_ref, cent_ref, g_ref, *, total):
+def finish_kernel(msg_ref, filt_ref, best_ref, cent_ref, g_ref, c_ref, sem, *, total):
     for p in range(PARTS):
         g_ref[4 * p:4 * p + 4, 0:C] = msg_ref[p, ROWS_OF:ROWS_OF + 4, :]
     row = lax.broadcasted_iota(jnp.int32, (C, C), 0)
@@ -404,25 +402,28 @@
             return dot(lhs, rhs, ((1,), (1,)))
         return dot(rhs, lhs, ((1,), (1,)))
 
+    sums = msg_ref[:, 0:ROWS_OF, :].reshape(K, C)
+    counts = jnp.concatenate(
+        [jnp.broadcast_to(msg_ref[p, ROWS_OF + 4:ROWS_OF + 5, :], (C, C)).T for p in range(0, PARTS, 4)],
+        axis=0,
+    )
+    c_ref[...] = times_inverse(sums, False) / (counts + 1.0)
+    copy = pltpu.make_async_copy(c_ref, cent_ref, sem)
+    copy.start()
     whitened_t = times_inverse(filt_ref[...], True)
     norms = jnp.sum(whitened_t * whitened_t, axis=0, keepdims=True)
     wh, wm, wl = split3(whitened_t)
     w_all = jnp.concatenate([wl, wm, wh, wm, wh, wh], axis=0)
-    best = None
-    for b in range(K // C):
-        sums = jnp.concatenate([msg_ref[4 * b + q, 0:ROWS_OF, :] for q in range(4)], axis=0)
-        counts = jnp.broadcast_to(msg_ref[4 * b, ROWS_OF + 4:ROWS_OF + 5, :], (C, C)).T
-        cent = times_inverse(sums, False) / (counts + 1.0)
-        cent_ref[b * C:(b + 1) * C, :] = cent
-        cent_norm = jnp.sum(cent * cent, axis=1, keepdims=True)
-        ch, cm, cl = split3(-2.0 * cent)
-        c_all = jnp.concatenate([ch, cm, cl, ch, cm, ch], axis=1)
-        value = dot(c_all, w_all, ((1,), (0,))) + cent_norm
-        low = jnp.min(value, axis=0, keepdims=True)
-        best = low if best is None else jnp.minimum(best, low)
+    cent = c_ref[...]
+    cent_norm = jnp.sum(cent * cent, axis=1, keepdims=True)
+    ch, cm, cl = split3(-2.0 * cent)
+    c_all = jnp.concatenate([ch, cm, cl, ch, cm, ch], axis=1)
+    value = dot(c_all, w_all, ((1,), (0,))) + cent_norm
+    best = jnp.min(value, axis=0, keepdims=True)
     result = (norms + best) / C
     for r in range(TH):
         best_ref[r:r + 1, :] = result[:, r * TW:(r + 1) * TW]
+    copy.wait()
 
 
 def run_finish(msg, filt, total):
@@ -433,7 +434,8 @@
             jax.ShapeDtypeStruct((TH, TW), F32),
             jax.ShapeDtypeStruct((K, C), F32),
         ),
-        scratch_shapes=[pltpu.VMEM((C, 2 * C), F32)],
+        out_specs=(VECTORS, pl.BlockSpec(memory_space=pltpu.HBM)),
+        scratch_shapes=[pltpu.VMEM((C, 2 * C), F32), pltpu.VMEM((K, C), F32), pltpu.SemaphoreType.DMA],
         compiler_params=pltpu.CompilerParams(vmem_limit_bytes=32 * 2**20),
     )(msg, filt)
 

time: 110 us -> 109 us (level)
  Pallas kernels: 17.1 us -> 15.7 us
    pallas_call x1, Pallas kernels: 7.76 us -> 6.43 us  [run_finish(): pl.pallas_call(functools.partial(finish_kernel, total=total), out_shape=(...]
where the time goes in v4:
time: 109 us; the launch traced here: 108 us
  blocking collectives  71.2 us (65%)
  Pallas kernels  15.7 us (14%)
  starting transfers between devices  13.3 us (12%)
  waiting for transfers between devices  4.62 us (4%)
  local copies, waits for them, and re-layouts  2.39 us (2%)
    all_to_all x4, blocking collectives, exchange(): return lax.all_to_all(x, axes, 0, 0)  65 us
    ppermute x2, starting transfers between devices, swap(): return (lax.ppermute(near, axes, near_pairs), far)  10.7 us
    pallas_call x1, Pallas kernels, run_finish(): pl.pallas_call(functools.partial(finish_kernel, total=total), out_shape=(...  6.43 us
    all_gather x1, blocking collectives, reduce_all(): return lax.all_gather(half, 'c', axis=0, tiled=True)  6.27 us
    ppermute x2, waiting for transfers between devices, swap(): far = lax.ppermute(far, axes, far_pairs)  4.61 us
    pallas_call x1, Pallas kernels, run_filter(): pl.pallas_call(filter_kernel, in_specs=[SCALARS] + [VECTORS] * 10, out_sh...  4.32 us
    pallas_call x1, Pallas kernels, run_prepare(): pl.pallas_call(prepare_kernel, out_shape=outs, in_specs=[SCALARS] + [VECT...  3.73 us
    ppermute x2, starting transfers between devices, swap(): far = lax.ppermute(far, axes, far_pairs)  2.58 us
  transfers between devices with their start and end apart: 4, of which 1 were waited for; matrix products, arithmetic and copies ran while one was open for 0% of the time, Pallas kernels for 3%

profile of v4, /device:TPU:1, one launch (start us, length us, event | category | flops | bytes accessed | tf_op | source)
XLA Modules:
  0.0 108.1 jit_solution(5339367613436891163)
XLA Ops:
  0.6 0.1 pad_add_fusion.odd_ref
  0.7 0.9 copy-done
  1.7 0.7 copy-done.1
  2.4 0.6 shard_map.50
  2.9 8.8 %collective-permute-start = (bf16[608,128]{1,0:T(8,128)(2,1)S(1)}, bf16[608,128]{1,0:T(8,128)(2,1)S(1)}, u32[]{:S(2)}, u32[]{:S(2)}) collective-permute-start(bf16[608,128]{1,0:T(8,128)(2,1)S(1)} %get-tuple-element.17), channel_id=1, source_target_pairs={{0,32},{32,0},{64,96},{96,64},{128,160},{160,128},{192,224},{224,1... | collective-permute-start | bytes 466952 | tf_op jit(solution)/shard_map/ppermute | solution.py:452
  11.7 1.9 %collective-permute-start.1 = (bf16[608,128]{1,0:T(8,128)(2,1)S(1)}, bf16[608,128]{1,0:T(8,128)(2,1)S(1)}, u32[]{:S(2)}, u32[]{:S(2)}) collective-permute-start(bf16[608,128]{1,0:T(8,128)(2,1)S(1)} %get-tuple-element.18), channel_id=1, source_target_pairs={{32,64},{96,128},{160,192},{224,256},{288,320},{352,384},{416,448}... | collective-permute-start | bytes 466952 | tf_op jit(solution)/shard_map/ppermute | solution.py:451
  13.7 0.0 collective-permute-done.row_near_ref
  13.7 4.6 %collective-permute-done.1.row_far_ref = bf16[608,128]{1,0:T(8,128)(2,1)S(1)} collective-permute-done((bf16[608,128]{1,0:T(8,128)(2,1)S(1)}, bf16[608,128]{1,0:T(8,128)(2,1)S(1)}, u32[]{:S(2)}, u32[]{:S(2)}) %collective-permute-start.1) | collective-permute-done | bytes 155680 | tf_op jit(solution)/shard_map/ppermute | solution.py:451
  18.3 0.7 shard_map.51
  19.0 1.9 %collective-permute-start.2 = (bf16[152,128]{1,0:T(8,128)(2,1)S(1)}, bf16[152,128]{1,0:T(8,128)(2,1)S(1)}, u32[]{:S(2)}, u32[]{:S(2)}) collective-permute-start(bf16[152,128]{1,0:T(8,128)(2,1)S(1)} %get-tuple-element.19), channel_id=1, source_target_pairs={{0,1},{1,0},{2,3},{3,2},{4,5},{5,4},{6,7},{7,6},{8,9},{9,8},{10,11... | collective-permute-start | bytes 116744 | tf_op jit(solution)/shard_map/ppermute | solution.py:452
  20.9 0.7 collective-permute-start.3
  21.6 0.0 copy-start.2
  21.6 0.7 copy-done.2
  22.2 3.7 %shard_map.52 = (bf16[1024,1024]{1,0:T(8,128)(2,1)S(1)}, f32[8,1024]{1,0:T(8,128)S(1)}, f32[16,160,128]{2,1,0:T(8,128)S(1)}, f32[16,160,128]{2,1,0:T(8,128)S(1)}...) custom-call(s32[2]{0:T(128)S(1)} %pad_add_fusion.odd_ref, ...), custom_call_target="tpu_custom_call" | custom-call | flops 134217728 | bytes 8388608 | tf_op jit(solution)/shard_map/pallas_call | solution.py:321
  26.0 0.0 collective-permute-done.2.col_near_ref
  26.0 0.0 collective-permute-done.3.col_far_ref
  26.0 4.3 %shard_map.53 = (f32[16,160,128]{2,1,0:T(8,128)S(1)}, f32[16,160,128]{2,1,0:T(8,128)S(1)}, f32[16,160,128]{2,1,0:T(8,128)S(1)}, f32[1024,128]{1,0:T(8,128)S(1)},...) custom-call(s32[2]{0:T(128)S(1)} %pad_add_fusion.odd_ref, ...), custom_call_target="tpu_custom_call", output_to_operand_aliasing={{0}: (6, {}), {1}: (7, {}), {2}: (8, {}), {3}: (9, {}), {4}... | custom-call | tf_op jit(solution)/shard_map/pallas_call | solution.py:332
  30.3 20.4 %all_to_all.20 = f32[32,40,128]{2,1,0:T(8,128)S(1)} all-to-all(f32[32,40,128]{2,1,0:T(8,128)S(1)} %get-tuple-element.30), channel_id=1, replica_groups=mesh['xh'=2,'y'=4,'c'=2,'zh'=4,'zl'=4,'xl'=2] {'c','xh','y','xl'}, dimensions={0} | all-to-all | bytes 1310720 | tf_op jit(solution)/shard_map/all_to_all | solution.py:456
  50.7 0.1 reduce_sum.27
  50.8 11.4 %all_to_all.21 = f32[4,40,128]{2,1,0:T(8,128)S(1)} all-to-all(f32[4,40,128]{2,1,0:T(8,128)S(1)} %broadcast_in_dim.6), channel_id=1, replica_groups=mesh['xh'=2,'y'=4,'c'=2,'zh'=4,'zl'=4,'xl'=2] {'zl'}, dimensions={0} | all-to-all | bytes 163840 | tf_op jit(solution)/shard_map/all_to_all | solution.py:456
  62.2 22.7 %all_to_all.22 = f32[4,40,128]{2,1,0:T(8,128)S(1)} all-to-all(f32[4,40,128]{2,1,0:T(8,128)S(1)} %broadcast_in_dim.7), channel_id=1, replica_groups=mesh['xh'=2,'y'=4,'c'=2,'zh'=4,'zl'=4,'xl'=2] {'zh'}, dimensions={0} | all-to-all | bytes 163840 | tf_op jit(solution)/shard_map/all_to_all | solution.py:456
  84.9 10.5 %all_to_all.23 = f32[16,40,128]{2,1,0:T(8,128)S(1)} all-to-all(f32[16,40,128]{2,1,0:T(8,128)S(1)} %broadcast_in_dim.8), channel_id=1, replica_groups=mesh['xh'=2,'y'=4,'c'=2,'zh'=4,'zl'=4,'xl'=2] {'xh','y','xl'}, dimensions={0} | all-to-all | bytes 655360 | tf_op jit(solution)/shard_map/all_to_all | solution.py:456
  95.4 6.3 %all_gather.3.msg_ref = f32[32,40,128]{2,1,0:T(8,128)S(1)} all-gather(f32[16,40,128]{2,1,0:T(8,128)S(1)} %all_to_all.23), channel_id=1, replica_groups=mesh['xh'=2,'y'=4,'c'=2,'zh'=4,'zl'=4,'xl'=2] {'c'}, dimensions={0}, use_global_device_ids=true | all-gather | bytes 983040 | tf_op jit(solution)/shard_map/all_gather | solution.py:468
  101.7 6.4 %shard_map.54 = (f32[8,128]{1,0:T(8,128)}, f32[1024,128]{1,0:T(8,128)}) custom-call(f32[32,40,128]{2,1,0:T(8,128)S(1)} %all_gather.3.msg_ref, f32[1024,128]{1,0:T(8,128)S(1)} %get-tuple-element.31.filt_ref), custom_call_target="tpu_custom_call" | custom-call | tf_op jit(solution)/shard_map/pallas_call | solution.py:431
  (7 shorter events, 0.1 us)
Async XLA Ops:
  0.7 1.0 copy-start
  1.7 0.7 copy-start.1
  2.9 10.7 %collective-permute-start = (bf16[608,128]{1,0:T(8,128)(2,1)S(1)}, bf16[608,128]{1,0:T(8,128)(2,1)S(1)}, u32[]{:S(2)}, u32[]{:S(2)}) collective-permute-start(bf16[608,128]{1,0:T(8,128)(2,1)S(1)} %get-tuple-element.17), channel_id=1, source_target_pairs={{0,32},{32,0},{64,96},{96,64},{128,160},{160,128},{192,224},{224,1... | collective-permute-start | bytes 466952 | tf_op jit(solution)/shard_map/ppermute | solution.py:452
  11.7 6.5 %collective-permute-start.1 = (bf16[608,128]{1,0:T(8,128)(2,1)S(1)}, bf16[608,128]{1,0:T(8,128)(2,1)S(1)}, u32[]{:S(2)}, u32[]{:S(2)}) collective-permute-start(bf16[608,128]{1,0:T(8,128)(2,1)S(1)} %get-tuple-element.18), channel_id=1, source_target_pairs={{32,64},{96,128},{160,192},{224,256},{288,320},{352,384},{416,448}... | collective-permute-start | bytes 466952 | tf_op jit(solution)/shard_map/ppermute | solution.py:451
  19.0 7.0 %collective-permute-start.2 = (bf16[152,128]{1,0:T(8,128)(2,1)S(1)}, bf16[152,128]{1,0:T(8,128)(2,1)S(1)}, u32[]{:S(2)}, u32[]{:S(2)}) collective-permute-start(bf16[152,128]{1,0:T(8,128)(2,1)S(1)} %get-tuple-element.19), channel_id=1, source_target_pairs={{0,1},{1,0},{2,3},{3,2},{4,5},{5,4},{6,7},{7,6},{8,9},{9,8},{10,11... | collective-permute-start | bytes 116744 | tf_op jit(solution)/shard_map/ppermute | solution.py:452
  20.9 5.1 %collective-permute-start.3 = (bf16[152,128]{1,0:T(8,128)(2,1)S(1)}, bf16[152,128]{1,0:T(8,128)(2,1)S(1)}, u32[]{:S(2)}, u32[]{:S(2)}) collective-permute-start(bf16[152,128]{1,0:T(8,128)(2,1)S(1)} %get-tuple-element.20), channel_id=1, source_target_pairs={{1,2},{3,4},{5,6},{7,8},{9,10},{11,12},{13,14},{15,16},{17,18},{19... | collective-permute-start | bytes 116744 | tf_op jit(solution)/shard_map/ppermute | solution.py:451
  21.6 0.7 copy-start.2

commit v5 on v4

--- a/solution.py
+++ b/solution.py
@@ -261,9 +261,9 @@
     gram = gram + (by_high[:, C:2 * C] + by_mid[:, :C])
     gram = gram + by_high[:, :C]
 
-    pieces = jnp.concatenate([high, mid, low], axis=1)
+    pieces = jnp.concatenate([high, mid], axis=1)
     part = dot(hot_ref[...], pieces, ((1,), (0,)))
-    part = (part[:, 2 * C:] + part[:, C:2 * C]) + part[:, :C]
+    part = part[:, C:] + part[:, :C]
     msg_ref[:, 0:ROWS_OF, :] = part.reshape(PARTS, ROWS_OF, C)
     msg_ref[:, ROWS_OF:ROWS_OF + 4, :] = gram.reshape(PARTS, 4, C)
     for p in range(PARTS):
@@ -412,12 +412,12 @@
     copy.start()
     whitened_t = times_inverse(filt_ref[...], True)
     norms = jnp.sum(whitened_t * whitened_t, axis=0, keepdims=True)
-    wh, wm, wl = split3(whitened_t)
-    w_all = jnp.concatenate([wl, wm, wh, wm, wh, wh], axis=0)
+    wh, wm, _ = split3(whitened_t)
+    w_all = jnp.concatenate([wm, wh, wh], axis=0)
     cent = c_ref[...]
     cent_norm = jnp.sum(cent * cent, axis=1, keepdims=True)
-    ch, cm, cl = split3(-2.0 * cent)
-    c_all = jnp.concatenate([ch, cm, cl, ch, cm, ch], axis=1)
+    ch, cm, _ = split3(-2.0 * cent)
+    c_all = jnp.concatenate([ch, cm, ch], axis=1)
     value = dot(c_all, w_all, ((1,), (0,))) + cent_norm
     best = jnp.min(value, axis=0, keepdims=True)
     result = (norms + best) / C

time: 109 us -> 107 us (0.982)
  Pallas kernels: 15.7 us -> 14.6 us
where the time goes in v5:
time: 107 us
  blocking collectives  71.2 us (67%)
  Pallas kernels  14.6 us (14%)
  starting transfers between devices  13.3 us (12%)
  waiting for transfers between devices  4.62 us (4%)
  local copies, waits for them, and re-layouts  2.39 us (2%)
    all_to_all x4, blocking collectives, exchange(): return lax.all_to_all(x, axes, 0, 0)  65 us
    ppermute x2, starting transfers between devices, swap(): return (lax.ppermute(near, axes, near_pairs), far)  10.7 us
    all_gather x1, blocking collectives, reduce_all(): return lax.all_gather(half, 'c', axis=0, tiled=True)  6.27 us
    pallas_call x1, Pallas kernels, run_finish(): pl.pallas_call(functools.partial(finish_kernel, total=total), out_shape=(...  5.89 us
    ppermute x2, waiting for transfers between devices, swap(): far = lax.ppermute(far, axes, far_pairs)  4.61 us
    pallas_call x1, Pallas kernels, run_filter(): pl.pallas_call(filter_kernel, in_specs=[SCALARS] + [VECTORS] * 10, out_sh...  3.78 us
    pallas_call x1, Pallas kernels, run_prepare(): pl.pallas_call(prepare_kernel, out_shape=outs, in_specs=[SCALARS] + [VECT...  3.73 us
    ppermute x2, starting transfers between devices, swap(): far = lax.ppermute(far, axes, far_pairs)  2.58 us
  transfers between devices with their start and end apart: 4, of which 1 were waited for; matrix products, arithmetic and copies ran while one was open for 0% of the time, Pallas kernels for 3%

profile of v5, /device:TPU:1, one launch (start us, length us, event | category | flops | bytes accessed | tf_op | source)
XLA Modules:
  0.0 107.0 jit_solution(5363422874991342301)
XLA Ops:
  0.6 0.1 pad_add_fusion.odd_ref
  0.7 0.9 copy-done
  1.7 0.7 copy-done.1
  2.4 0.6 shard_map.50
  2.9 8.8 %collective-permute-start = (bf16[608,128]{1,0:T(8,128)(2,1)S(1)}, bf16[608,128]{1,0:T(8,128)(2,1)S(1)}, u32[]{:S(2)}, u32[]{:S(2)}) collective-permute-start(bf16[608,128]{1,0:T(8,128)(2,1)S(1)} %get-tuple-element.17), channel_id=1, source_target_pairs={{0,32},{32,0},{64,96},{96,64},{128,160},{160,128},{192,224},{224,1... | collective-permute-start | bytes 466952 | tf_op jit(solution)/shard_map/ppermute | solution.py:452
  11.7 1.9 %collective-permute-start.1 = (bf16[608,128]{1,0:T(8,128)(2,1)S(1)}, bf16[608,128]{1,0:T(8,128)(2,1)S(1)}, u32[]{:S(2)}, u32[]{:S(2)}) collective-permute-start(bf16[608,128]{1,0:T(8,128)(2,1)S(1)} %get-tuple-element.18), channel_id=1, source_target_pairs={{32,64},{96,128},{160,192},{224,256},{288,320},{352,384},{416,448}... | collective-permute-start | bytes 466952 | tf_op jit(solution)/shard_map/ppermute | solution.py:451
  13.7 0.0 collective-permute-done.row_near_ref
  13.7 4.6 %collective-permute-done.1.row_far_ref = bf16[608,128]{1,0:T(8,128)(2,1)S(1)} collective-permute-done((bf16[608,128]{1,0:T(8,128)(2,1)S(1)}, bf16[608,128]{1,0:T(8,128)(2,1)S(1)}, u32[]{:S(2)}, u32[]{:S(2)}) %collective-permute-start.1) | collective-permute-done | bytes 155680 | tf_op jit(solution)/shard_map/ppermute | solution.py:451
  18.3 0.7 shard_map.51
  19.0 1.9 %collective-permute-start.2 = (bf16[152,128]{1,0:T(8,128)(2,1)S(1)}, bf16[152,128]{1,0:T(8,128)(2,1)S(1)}, u32[]{:S(2)}, u32[]{:S(2)}) collective-permute-start(bf16[152,128]{1,0:T(8,128)(2,1)S(1)} %get-tuple-element.19), channel_id=1, source_target_pairs={{0,1},{1,0},{2,3},{3,2},{4,5},{5,4},{6,7},{7,6},{8,9},{9,8},{10,11... | collective-permute-start | bytes 116744 | tf_op jit(solution)/shard_map/ppermute | solution.py:452
  20.9 0.7 collective-permute-start.3
  21.6 0.0 copy-start.2
  21.6 0.7 copy-done.2
  22.2 3.7 %shard_map.52 = (bf16[1024,1024]{1,0:T(8,128)(2,1)S(1)}, f32[8,1024]{1,0:T(8,128)S(1)}, f32[16,160,128]{2,1,0:T(8,128)S(1)}, f32[16,160,128]{2,1,0:T(8,128)S(1)}...) custom-call(s32[2]{0:T(128)S(1)} %pad_add_fusion.odd_ref, ...), custom_call_target="tpu_custom_call" | custom-call | flops 134217728 | bytes 8388608 | tf_op jit(solution)/shard_map/pallas_call | solution.py:321
  26.0 0.0 collective-permute-done.2.col_near_ref
  26.0 0.0 collective-permute-done.3.col_far_ref
  26.0 3.8 %shard_map.53 = (f32[16,160,128]{2,1,0:T(8,128)S(1)}, f32[16,160,128]{2,1,0:T(8,128)S(1)}, f32[16,160,128]{2,1,0:T(8,128)S(1)}, f32[1024,128]{1,0:T(8,128)S(1)},...) custom-call(s32[2]{0:T(128)S(1)} %pad_add_fusion.odd_ref, ...), custom_call_target="tpu_custom_call", output_to_operand_aliasing={{0}: (6, {}), {1}: (7, {}), {2}: (8, {}), {3}: (9, {}), {4}... | custom-call | tf_op jit(solution)/shard_map/pallas_call | solution.py:332
  29.8 20.4 %all_to_all.20 = f32[32,40,128]{2,1,0:T(8,128)S(1)} all-to-all(f32[32,40,128]{2,1,0:T(8,128)S(1)} %get-tuple-element.30), channel_id=1, replica_groups=mesh['xh'=2,'y'=4,'c'=2,'zh'=4,'zl'=4,'xl'=2] {'c','xh','y','xl'}, dimensions={0} | all-to-all | bytes 1310720 | tf_op jit(solution)/shard_map/all_to_all | solution.py:456
  50.2 0.1 reduce_sum.27
  50.3 11.4 %all_to_all.21 = f32[4,40,128]{2,1,0:T(8,128)S(1)} all-to-all(f32[4,40,128]{2,1,0:T(8,128)S(1)} %broadcast_in_dim.6), channel_id=1, replica_groups=mesh['xh'=2,'y'=4,'c'=2,'zh'=4,'zl'=4,'xl'=2] {'zl'}, dimensions={0} | all-to-all | bytes 163840 | tf_op jit(solution)/shard_map/all_to_all | solution.py:456
  61.7 22.7 %all_to_all.22 = f32[4,40,128]{2,1,0:T(8,128)S(1)} all-to-all(f32[4,40,128]{2,1,0:T(8,128)S(1)} %broadcast_in_dim.7), channel_id=1, replica_groups=mesh['xh'=2,'y'=4,'c'=2,'zh'=4,'zl'=4,'xl'=2] {'zh'}, dimensions={0} | all-to-all | bytes 163840 | tf_op jit(solution)/shard_map/all_to_all | solution.py:456
  84.4 10.5 %all_to_all.23 = f32[16,40,128]{2,1,0:T(8,128)S(1)} all-to-all(f32[16,40,128]{2,1,0:T(8,128)S(1)} %broadcast_in_dim.8), channel_id=1, replica_groups=mesh['xh'=2,'y'=4,'c'=2,'zh'=4,'zl'=4,'xl'=2] {'xh','y','xl'}, dimensions={0} | all-to-all | bytes 655360 | tf_op jit(solution)/shard_map/all_to_all | solution.py:456
  94.9 6.3 %all_gather.3.msg_ref = f32[32,40,128]{2,1,0:T(8,128)S(1)} all-gather(f32[16,40,128]{2,1,0:T(8,128)S(1)} %all_to_all.23), channel_id=1, replica_groups=mesh['xh'=2,'y'=4,'c'=2,'zh'=4,'zl'=4,'xl'=2] {'c'}, dimensions={0}, use_global_device_ids=true | all-gather | bytes 983040 | tf_op jit(solution)/shard_map/all_gather | solution.py:468
  101.2 5.9 %shard_map.54 = (f32[8,128]{1,0:T(8,128)}, f32[1024,128]{1,0:T(8,128)}) custom-call(f32[32,40,128]{2,1,0:T(8,128)S(1)} %all_gather.3.msg_ref, f32[1024,128]{1,0:T(8,128)S(1)} %get-tuple-element.31.filt_ref), custom_call_target="tpu_custom_call" | custom-call | tf_op jit(solution)/shard_map/pallas_call | solution.py:431
  (7 shorter events, 0.1 us)
Async XLA Ops:
  0.7 1.0 copy-start
  1.7 0.7 copy-start.1
  2.9 10.7 %collective-permute-start = (bf16[608,128]{1,0:T(8,128)(2,1)S(1)}, bf16[608,128]{1,0:T(8,128)(2,1)S(1)}, u32[]{:S(2)}, u32[]{:S(2)}) collective-permute-start(bf16[608,128]{1,0:T(8,128)(2,1)S(1)} %get-tuple-element.17), channel_id=1, source_target_pairs={{0,32},{32,0},{64,96},{96,64},{128,160},{160,128},{192,224},{224,1... | collective-permute-start | bytes 466952 | tf_op jit(solution)/shard_map/ppermute | solution.py:452
  11.7 6.5 %collective-permute-start.1 = (bf16[608,128]{1,0:T(8,128)(2,1)S(1)}, bf16[608,128]{1,0:T(8,128)(2,1)S(1)}, u32[]{:S(2)}, u32[]{:S(2)}) collective-permute-start(bf16[608,128]{1,0:T(8,128)(2,1)S(1)} %get-tuple-element.18), channel_id=1, source_target_pairs={{32,64},{96,128},{160,192},{224,256},{288,320},{352,384},{416,448}... | collective-permute-start | bytes 466952 | tf_op jit(solution)/shard_map/ppermute | solution.py:451
  19.0 7.0 %collective-permute-start.2 = (bf16[152,128]{1,0:T(8,128)(2,1)S(1)}, bf16[152,128]{1,0:T(8,128)(2,1)S(1)}, u32[]{:S(2)}, u32[]{:S(2)}) collective-permute-start(bf16[152,128]{1,0:T(8,128)(2,1)S(1)} %get-tuple-element.19), channel_id=1, source_target_pairs={{0,1},{1,0},{2,3},{3,2},{4,5},{5,4},{6,7},{7,6},{8,9},{9,8},{10,11... | collective-permute-start | bytes 116744 | tf_op jit(solution)/shard_map/ppermute | solution.py:452
  20.9 5.1 %collective-permute-start.3 = (bf16[152,128]{1,0:T(8,128)(2,1)S(1)}, bf16[152,128]{1,0:T(8,128)(2,1)S(1)}, u32[]{:S(2)}, u32[]{:S(2)}) collective-permute-start(bf16[152,128]{1,0:T(8,128)(2,1)S(1)} %get-tuple-element.20), channel_id=1, source_target_pairs={{1,2},{3,4},{5,6},{7,8},{9,10},{11,12},{13,14},{15,16},{17,18},{19... | collective-permute-start | bytes 116744 | tf_op jit(solution)/shard_map/ppermute | solution.py:451
  21.6 0.7 copy-start.2

commit v6 on v5

--- a/solution.py
+++ b/solution.py
@@ -448,8 +448,8 @@
     near_pairs = [(i, i ^ 1) for i in range(size)]
     far_pairs = [(i, i + 1) for i in range(1, size - 1, 2)]
     far_pairs = far_pairs + [(b, a) for a, b in far_pairs]
-    far = lax.ppermute(far, axes, far_pairs)
-    return lax.ppermute(near, axes, near_pairs), far
+    near = lax.ppermute(near, axes, near_pairs)
+    return near, lax.ppermute(far, axes, far_pairs)
 
 
 def exchange(x, axes):

time: 107 us -> 107 us (level)
  no operation moved by 1% of the time
where the time goes in v6:
time: 107 us
  blocking collectives  71.2 us (67%)
  Pallas kernels  14.6 us (14%)
  starting transfers between devices  13.3 us (12%)
  waiting for transfers between devices  4.62 us (4%)
  local copies, waits for them, and re-layouts  2.39 us (2%)
    all_to_all x4, blocking collectives, exchange(): return lax.all_to_all(x, axes, 0, 0)  65 us
    ppermute x2, starting transfers between devices, swap(): near = lax.ppermute(near, axes, near_pairs)  10.7 us
    all_gather x1, blocking collectives, reduce_all(): return lax.all_gather(half, 'c', axis=0, tiled=True)  6.27 us
    pallas_call x1, Pallas kernels, run_finish(): pl.pallas_call(functools.partial(finish_kernel, total=total), out_shape=(...  5.89 us
    ppermute x2, waiting for transfers between devices, swap(): return (near, lax.ppermute(far, axes, far_pairs))  4.61 us
    pallas_call x1, Pallas kernels, run_filter(): pl.pallas_call(filter_kernel, in_specs=[SCALARS] + [VECTORS] * 10, out_sh...  3.78 us
    pallas_call x1, Pallas kernels, run_prepare(): pl.pallas_call(prepare_kernel, out_shape=outs, in_specs=[SCALARS] + [VECT...  3.73 us
    ppermute x2, starting transfers between devices, swap(): return (near, lax.ppermute(far, axes, far_pairs))  2.58 us
  transfers between devices with their start and end apart: 4, of which 1 were waited for; matrix products, arithmetic and copies ran while one was open for 0% of the time, Pallas kernels for 3%

profile of v6, /device:TPU:1, one launch (start us, length us, event | category | flops | bytes accessed | tf_op | source)
XLA Modules:
  0.0 107.0 jit_solution(5363422874991342301)
XLA Ops:
  0.6 0.1 pad_add_fusion.odd_ref
  0.7 0.9 copy-done
  1.7 0.7 copy-done.1
  2.4 0.6 shard_map.50
  2.9 8.8 %collective-permute-start = (bf16[608,128]{1,0:T(8,128)(2,1)S(1)}, bf16[608,128]{1,0:T(8,128)(2,1)S(1)}, u32[]{:S(2)}, u32[]{:S(2)}) collective-permute-start(bf16[608,128]{1,0:T(8,128)(2,1)S(1)} %get-tuple-element.17), channel_id=1, source_target_pairs={{0,32},{32,0},{64,96},{96,64},{128,160},{160,128},{192,224},{224,1... | collective-permute-start | bytes 466952 | tf_op jit(solution)/shard_map/ppermute | solution.py:451
  11.7 1.9 %collective-permute-start.1 = (bf16[608,128]{1,0:T(8,128)(2,1)S(1)}, bf16[608,128]{1,0:T(8,128)(2,1)S(1)}, u32[]{:S(2)}, u32[]{:S(2)}) collective-permute-start(bf16[608,128]{1,0:T(8,128)(2,1)S(1)} %get-tuple-element.18), channel_id=1, source_target_pairs={{32,64},{96,128},{160,192},{224,256},{288,320},{352,384},{416,448}... | collective-permute-start | bytes 466952 | tf_op jit(solution)/shard_map/ppermute | solution.py:452
  13.7 0.0 collective-permute-done.row_near_ref
  13.7 4.6 %collective-permute-done.1.row_far_ref = bf16[608,128]{1,0:T(8,128)(2,1)S(1)} collective-permute-done((bf16[608,128]{1,0:T(8,128)(2,1)S(1)}, bf16[608,128]{1,0:T(8,128)(2,1)S(1)}, u32[]{:S(2)}, u32[]{:S(2)}) %collective-permute-start.1) | collective-permute-done | bytes 155680 | tf_op jit(solution)/shard_map/ppermute | solution.py:452
  18.3 0.7 shard_map.51
  19.0 1.9 %collective-permute-start.2 = (bf16[152,128]{1,0:T(8,128)(2,1)S(1)}, bf16[152,128]{1,0:T(8,128)(2,1)S(1)}, u32[]{:S(2)}, u32[]{:S(2)}) collective-permute-start(bf16[152,128]{1,0:T(8,128)(2,1)S(1)} %get-tuple-element.19), channel_id=1, source_target_pairs={{0,1},{1,0},{2,3},{3,2},{4,5},{5,4},{6,7},{7,6},{8,9},{9,8},{10,11... | collective-permute-start | bytes 116744 | tf_op jit(solution)/shard_map/ppermute | solution.py:451
  20.9 0.7 collective-permute-start.3
  21.6 0.0 copy-start.2
  21.6 0.7 copy-done.2
  22.2 3.7 %shard_map.52 = (bf16[1024,1024]{1,0:T(8,128)(2,1)S(1)}, f32[8,1024]{1,0:T(8,128)S(1)}, f32[16,160,128]{2,1,0:T(8,128)S(1)}, f32[16,160,128]{2,1,0:T(8,128)S(1)}...) custom-call(s32[2]{0:T(128)S(1)} %pad_add_fusion.odd_ref, ...), custom_call_target="tpu_custom_call" | custom-call | flops 134217728 | bytes 8388608 | tf_op jit(solution)/shard_map/pallas_call | solution.py:321
  26.0 0.0 collective-permute-done.2.col_near_ref
  26.0 0.0 collective-permute-done.3.col_far_ref
  26.0 3.8 %shard_map.53 = (f32[16,160,128]{2,1,0:T(8,128)S(1)}, f32[16,160,128]{2,1,0:T(8,128)S(1)}, f32[16,160,128]{2,1,0:T(8,128)S(1)}, f32[1024,128]{1,0:T(8,128)S(1)},...) custom-call(s32[2]{0:T(128)S(1)} %pad_add_fusion.odd_ref, ...), custom_call_target="tpu_custom_call", output_to_operand_aliasing={{0}: (6, {}), {1}: (7, {}), {2}: (8, {}), {3}: (9, {}), {4}... | custom-call | tf_op jit(solution)/shard_map/pallas_call | solution.py:332
  29.8 20.4 %all_to_all.20 = f32[32,40,128]{2,1,0:T(8,128)S(1)} all-to-all(f32[32,40,128]{2,1,0:T(8,128)S(1)} %get-tuple-element.30), channel_id=1, replica_groups=mesh['xh'=2,'y'=4,'c'=2,'zh'=4,'zl'=4,'xl'=2] {'c','xh','y','xl'}, dimensions={0} | all-to-all | bytes 1310720 | tf_op jit(solution)/shard_map/all_to_all | solution.py:456
  50.2 0.1 reduce_sum.27
  50.3 11.4 %all_to_all.21 = f32[4,40,128]{2,1,0:T(8,128)S(1)} all-to-all(f32[4,40,128]{2,1,0:T(8,128)S(1)} %broadcast_in_dim.6), channel_id=1, replica_groups=mesh['xh'=2,'y'=4,'c'=2,'zh'=4,'zl'=4,'xl'=2] {'zl'}, dimensions={0} | all-to-all | bytes 163840 | tf_op jit(solution)/shard_map/all_to_all | solution.py:456
  61.7 22.7 %all_to_all.22 = f32[4,40,128]{2,1,0:T(8,128)S(1)} all-to-all(f32[4,40,128]{2,1,0:T(8,128)S(1)} %broadcast_in_dim.7), channel_id=1, replica_groups=mesh['xh'=2,'y'=4,'c'=2,'zh'=4,'zl'=4,'xl'=2] {'zh'}, dimensions={0} | all-to-all | bytes 163840 | tf_op jit(solution)/shard_map/all_to_all | solution.py:456
  84.4 10.5 %all_to_all.23 = f32[16,40,128]{2,1,0:T(8,128)S(1)} all-to-all(f32[16,40,128]{2,1,0:T(8,128)S(1)} %broadcast_in_dim.8), channel_id=1, replica_groups=mesh['xh'=2,'y'=4,'c'=2,'zh'=4,'zl'=4,'xl'=2] {'xh','y','xl'}, dimensions={0} | all-to-all | bytes 655360 | tf_op jit(solution)/shard_map/all_to_all | solution.py:456
  94.9 6.3 %all_gather.3.msg_ref = f32[32,40,128]{2,1,0:T(8,128)S(1)} all-gather(f32[16,40,128]{2,1,0:T(8,128)S(1)} %all_to_all.23), channel_id=1, replica_groups=mesh['xh'=2,'y'=4,'c'=2,'zh'=4,'zl'=4,'xl'=2] {'c'}, dimensions={0}, use_global_device_ids=true | all-gather | bytes 983040 | tf_op jit(solution)/shard_map/all_gather | solution.py:468
  101.2 5.9 %shard_map.54 = (f32[8,128]{1,0:T(8,128)}, f32[1024,128]{1,0:T(8,128)}) custom-call(f32[32,40,128]{2,1,0:T(8,128)S(1)} %all_gather.3.msg_ref, f32[1024,128]{1,0:T(8,128)S(1)} %get-tuple-element.31.filt_ref), custom_call_target="tpu_custom_call" | custom-call | tf_op jit(solution)/shard_map/pallas_call | solution.py:431
  (7 shorter events, 0.1 us)
Async XLA Ops:
  0.7 1.0 copy-start
  1.7 0.7 copy-start.1
  2.9 10.7 %collective-permute-start = (bf16[608,128]{1,0:T(8,128)(2,1)S(1)}, bf16[608,128]{1,0:T(8,128)(2,1)S(1)}, u32[]{:S(2)}, u32[]{:S(2)}) collective-permute-start(bf16[608,128]{1,0:T(8,128)(2,1)S(1)} %get-tuple-element.17), channel_id=1, source_target_pairs={{0,32},{32,0},{64,96},{96,64},{128,160},{160,128},{192,224},{224,1... | collective-permute-start | bytes 466952 | tf_op jit(solution)/shard_map/ppermute | solution.py:451
  11.7 6.5 %collective-permute-start.1 = (bf16[608,128]{1,0:T(8,128)(2,1)S(1)}, bf16[608,128]{1,0:T(8,128)(2,1)S(1)}, u32[]{:S(2)}, u32[]{:S(2)}) collective-permute-start(bf16[608,128]{1,0:T(8,128)(2,1)S(1)} %get-tuple-element.18), channel_id=1, source_target_pairs={{32,64},{96,128},{160,192},{224,256},{288,320},{352,384},{416,448}... | collective-permute-start | bytes 466952 | tf_op jit(solution)/shard_map/ppermute | solution.py:452
  19.0 7.0 %collective-permute-start.2 = (bf16[152,128]{1,0:T(8,128)(2,1)S(1)}, bf16[152,128]{1,0:T(8,128)(2,1)S(1)}, u32[]{:S(2)}, u32[]{:S(2)}) collective-permute-start(bf16[152,128]{1,0:T(8,128)(2,1)S(1)} %get-tuple-element.19), channel_id=1, source_target_pairs={{0,1},{1,0},{2,3},{3,2},{4,5},{5,4},{6,7},{7,6},{8,9},{9,8},{10,11... | collective-permute-start | bytes 116744 | tf_op jit(solution)/shard_map/ppermute | solution.py:451
  20.9 5.1 %collective-permute-start.3 = (bf16[152,128]{1,0:T(8,128)(2,1)S(1)}, bf16[152,128]{1,0:T(8,128)(2,1)S(1)}, u32[]{:S(2)}, u32[]{:S(2)}) collective-permute-start(bf16[152,128]{1,0:T(8,128)(2,1)S(1)} %get-tuple-element.20), channel_id=1, source_target_pairs={{1,2},{3,4},{5,6},{7,8},{9,10},{11,12},{13,14},{15,16},{17,18},{19... | collective-permute-start | bytes 116744 | tf_op jit(solution)/shard_map/ppermute | solution.py:452
  21.6 0.7 copy-start.2
